TPU v7x, 256 devices: a whole 4x4x8 slice. The times are simulated.
256 devices in a mesh: section: 32 (over x, z), dp: 8 (over y, core).
Axes of the slice: x: 4, y: 4, z: 8, core: 2. Of those that a mesh axis runs over, the one named last changes fastest.
Arguments:
- inputs: bfloat16 [8, 256, 512], P(None, 'dp'), may hold values from -6 to 6
- targets: bfloat16 [8, 256, 512], P(None, 'dp'), may hold values from -6 to 6
- w_in: bfloat16 [32, 512, 4096], P('section'), may hold values from -0.25 to 0.25
- w_out: bfloat16 [32, 4096, 512], P('section'), may hold values from -0.0234375 to 0.0234375
Outputs:
- grad_w_in: float32 [32, 512, 4096], P('section', None, 'dp')
- grad_w_out: float32 [32, 4096, 512], P('section', 'dp')
All inputs are finite; a program needn't handle non-finite values.
Results may differ from a plain program's by a relative error of at most 0.019.
Values may be sent and summed in bfloat16 or wider, within the bound.
No kernel may reach another device: no remote copies, remote signals or barrier semaphores. Data moves between devices by JAX's collectives and lax.ppermute only.
A program may use at most 64 MiB of HBM per device.

v0:
```python
import math

import jax
import jax.numpy as jnp
from jax import lax
from jax.sharding import PartitionSpec as P


def from_behind(value, axis, by):
    size = lax.axis_size(axis)
    pairs = [(i, i + by) for i in range(size) if 0 <= i + by < size]
    return lax.ppermute(value, axis, pairs)


def read_slot(buffer, slot_idx):
    return lax.dynamic_index_in_dim(buffer, slot_idx, 0, keepdims=False)


def store_slot(buffer, value, slot_idx, is_valid):
    chosen = jnp.where(is_valid, value, read_slot(buffer, slot_idx))
    return lax.dynamic_update_index_in_dim(buffer, chosen, slot_idx, 0)


def per_device(inputs, targets, w_in, w_out):
    section_count = lax.axis_size("section")
    section_idx = lax.axis_index("section")
    micro_count, row_count, feature_dim = inputs.shape
    hidden_dim = w_in.shape[2]
    loss_scale = 1.0 / math.sqrt(micro_count * row_count * lax.axis_size("dp"))
    weight_in = w_in[0]
    weight_out = w_out[0]
    tick_count = micro_count + section_count - 1
    is_first = section_idx == 0
    is_last = section_idx == section_count - 1
    zero_rows = jnp.zeros((row_count, feature_dim), jnp.bfloat16)
    zero_hidden = jnp.zeros((row_count, hidden_dim), jnp.bfloat16)

    def apply_cell(act_in):
        pre_act = jnp.dot(act_in, weight_in, preferred_element_type=jnp.float32)
        hidden = (pre_act * jax.nn.sigmoid(pre_act)).astype(jnp.bfloat16)
        act_out = (
            act_in.astype(jnp.float32)
            + jnp.dot(hidden, weight_out, preferred_element_type=jnp.float32)
        ).astype(jnp.bfloat16)
        return (hidden, act_out)

    def bypass_cell(act_in):
        return (zero_hidden, act_in)

    def forward_tick(carry_in, tick_num):
        received, stash_act, stash_hidden, grad_last = carry_in
        slot_num = tick_num - section_idx
        is_valid = (slot_num >= 0) & (slot_num < micro_count)
        slot_idx = jnp.clip(slot_num, 0, micro_count - 1)
        act_in = jnp.where(is_first, read_slot(inputs, slot_idx), received)
        hidden, act_out = lax.cond(is_valid, apply_cell, bypass_cell, act_in)
        target_now = read_slot(targets, slot_idx)
        grad_top = (
            (act_out.astype(jnp.float32) - target_now.astype(jnp.float32)) * loss_scale
        ).astype(jnp.bfloat16)
        stash_act = store_slot(stash_act, act_in, slot_idx, is_valid)
        stash_hidden = store_slot(stash_hidden, hidden, slot_idx, is_valid)
        grad_last = store_slot(grad_last, grad_top, slot_idx, is_valid & is_last)
        sent_on = from_behind(act_out, "section", 1)
        return ((sent_on, stash_act, stash_hidden, grad_last), None)

    hidden_init = jnp.zeros((micro_count, row_count, hidden_dim), jnp.bfloat16)
    forward_init = (zero_rows, jnp.zeros_like(inputs), hidden_init, jnp.zeros_like(inputs))
    (unused_act, stash_act, stash_hidden, grad_last), unused_out = lax.scan(
        forward_tick, forward_init, jnp.arange(tick_count, dtype=jnp.int32)
    )

    def backward_work(operands):
        act_in, grad_y = operands
        pre_act = jnp.dot(act_in, weight_in, preferred_element_type=jnp.float32)
        sigma = jax.nn.sigmoid(pre_act)
        slope = sigma + pre_act * sigma * (1.0 - sigma)
        through = jnp.dot(grad_y, weight_out.T, preferred_element_type=jnp.float32)
        grad_pre = (through * slope).astype(jnp.bfloat16)
        grad_x = (
            grad_y.astype(jnp.float32)
            + jnp.dot(grad_pre, weight_in.T, preferred_element_type=jnp.float32)
        ).astype(jnp.bfloat16)
        return (grad_pre, grad_x)

    def bypass_back(operands):
        return (zero_hidden, zero_rows)

    def backward_tick(carry_in, tick_num):
        received, stash_grad, stash_pre = carry_in
        slot_num = tick_num - (section_count - 1 - section_idx)
        is_valid = (slot_num >= 0) & (slot_num < micro_count)
        slot_idx = jnp.clip(slot_num, 0, micro_count - 1)
        grad_y = jnp.where(is_last, read_slot(grad_last, slot_idx), received)
        operands = (read_slot(stash_act, slot_idx), grad_y)
        grad_pre, grad_x = lax.cond(is_valid, backward_work, bypass_back, operands)
        stash_grad = store_slot(stash_grad, grad_y, slot_idx, is_valid)
        stash_pre = store_slot(stash_pre, grad_pre, slot_idx, is_valid)
        sent_back = from_behind(grad_x, "section", -1)
        return ((sent_back, stash_grad, stash_pre), None)

    backward_init = (zero_rows, jnp.zeros_like(inputs), hidden_init)
    (unused_grad, stash_grad, stash_pre), unused_more = lax.scan(
        backward_tick, backward_init, jnp.arange(tick_count, dtype=jnp.int32)
    )
    all_act = stash_act.reshape(micro_count * row_count, feature_dim)
    all_grad = stash_grad.reshape(micro_count * row_count, feature_dim)
    all_hidden = stash_hidden.reshape(micro_count * row_count, hidden_dim)
    all_pre = stash_pre.reshape(micro_count * row_count, hidden_dim)
    total_in = jnp.einsum("rd,rf->df", all_act, all_pre, preferred_element_type=jnp.float32)
    total_out = jnp.einsum("rf,rd->fd", all_hidden, all_grad, preferred_element_type=jnp.float32)
    share_in, share_out = (
        lax.psum_scatter(
            total_in.astype(jnp.bfloat16), "dp", scatter_dimension=1, tiled=True
        ).astype(jnp.float32),
        lax.psum_scatter(
            total_out.astype(jnp.bfloat16), "dp", scatter_dimension=0, tiled=True
        ).astype(jnp.float32),
    )
    return (share_in[None], share_out[None])


def solution(mesh):
    in_specs = (
        P(None, "dp", None),
        P(None, "dp", None),
        P("section", None, None),
        P("section", None, None),
    )
    out_specs = (P("section", None, "dp"), P("section", "dp", None))
    return jax.shard_map(
        per_device, mesh=mesh, in_specs=in_specs, out_specs=out_specs, check_vma=False
    )
```

profile of v0, /device:TPU:1, one launch (start us, length us, event | category | flops | bytes accessed | tf_op | source)
XLA Modules:
  0.0 1185.0 jit_solution(4318011105973288437)
XLA Ops:
  7.5 406.8 %while.32 = (s32[]{:T(128)}, bf16[32,512]{1,0:T(8,128)(2,1)S(1)}, bf16[8,32,512]{2,1,0:T(8,128)(2,1)S(1)}, bf16[8,32,4096]{2,1,0:T(8,128)(2,1)S(1)}, bf16[8,32,5...) while((s32[]{:T(128)}, bf16[32,512]{1,0:T(8,128)(2,1)S(1)}, ...), condition=%wide.region_3.4_spmd, body=%wide.region_0.3_spmd.sunk | while | flops 269402112 | bytes 27656560 | solution.py:69
  108.1 7.7 collective-permute-start
  128.2 8.9 collective-permute-start
  149.5 8.9 collective-permute-start
  170.9 8.9 collective-permute-start
  192.3 6.2 collective-permute-start
  210.9 5.8 collective-permute-start
  229.0 8.5 collective-permute-start
  241.3 5.7 collective-permute-start
  251.0 9.6 collective-permute-start
  331.2 5.9 collective-permute-start
  359.9 5.8 collective-permute-start
  416.0 610.3 %while.33 = (s32[]{:T(128)}, bf16[32,512]{1,0:T(8,128)(2,1)S(1)}, bf16[8,32,512]{2,1,0:T(8,128)(2,1)S(1)}, bf16[8,32,4096]{2,1,0:T(8,128)(2,1)}, s32[39]{0:T(128...) while((s32[]{:T(128)}, bf16[32,512]{1,0:T(8,128)(2,1)S(1)}, ...), condition=%wide.region_7.8_spmd, body=%wide.region_4.7_spmd.sunk | while | flops 404045824 | bytes 49513344 | solution.py:103
  688.7 212.0 %collective-permute-done.1 = bf16[32,512]{1,0:T(8,128)(2,1)S(1)} collective-permute-done((bf16[32,512]{1,0:T(8,128)(2,1)S(1)}, bf16[32,512]{1,0:T(8,128)(2,1)S(1)}, u32[]{:S(2)}, u32[]{:S(2)}) %collective-permute-start.1) | collective-permute-done | bytes 32800 | tf_op jit(solution)/shard_map/while/body/eval_jaxpr/ppermute | solution.py:12
  902.0 7.8 conditional.5
  917.9 7.8 conditional.5
  933.8 7.8 conditional.5
  950.2 7.8 conditional.5
  966.1 7.8 conditional.5
  982.3 7.8 conditional.5
  998.5 7.8 conditional.5
  1013.8 7.8 conditional.5
  1034.4 99.6 %reduce-scatter.5.cloned.1.call-done = bf16[512,512]{1,0:T(8,128)(2,1)} async-done(((bf16[4096,512]{1,0:T(8,128)(2,1)}), bf16[512,512]{1,0:T(8,128)(2,1)}) %reduce-scatter.5.cloned.1.call-update) | async-done | bytes 524304 | tf_op jit(solution)/shard_map/reduce_scatter | solution.py:116
  1136.1 39.9 %reduce-scatter.3.cloned.1.call-done = bf16[512,512]{1,0:T(8,128)(2,1)} async-done(((bf16[512,4096]{1,0:T(8,128)(2,1)}), bf16[512,512]{1,0:T(8,128)(2,1)}) %reduce-scatter.3.cloned.1.call-update) | async-done | bytes 524304 | tf_op jit(solution)/shard_map/reduce_scatter | solution.py:113
  (882 shorter events, 772.3 us)
Async XLA Ops:
  7.2 1126.8 %reduce-scatter.5.cloned.1.call-start = ((), (), s32[]{:S(2)}) async-start(), calls=%async_computation.3 | async-start | bytes 4718592 | tf_op jit(solution)/shard_map/reduce_scatter | solution.py:116
  108.1 8.7 collective-permute-start
  128.2 10.0 collective-permute-start
  149.5 9.9 collective-permute-start
  170.9 9.9 collective-permute-start
  192.3 7.2 collective-permute-start
  229.0 9.5 collective-permute-start
  251.0 10.6 collective-permute-start
  418.0 7.0 collective-permute-start.1
  427.1 7.2 collective-permute-start.1
  436.4 7.1 collective-permute-start.1
  445.5 7.1 collective-permute-start.1
  454.6 7.2 collective-permute-start.1
  463.9 7.2 collective-permute-start.1
  473.1 7.0 collective-permute-start.1
  482.2 7.0 collective-permute-start.1
  491.3 7.2 collective-permute-start.1
  544.1 7.3 collective-permute-start.1
  632.3 7.1 collective-permute-start.1
  658.7 7.0 collective-permute-start.1
  685.7 215.1 %collective-permute-start.1 = (bf16[32,512]{1,0:T(8,128)(2,1)S(1)}, bf16[32,512]{1,0:T(8,128)(2,1)S(1)}, u32[]{:S(2)}, u32[]{:S(2)}) collective-permute-start(bf16[32,512]{1,0:T(8,128)(2,1)S(1)} %get-tuple-element.457), channel_id=1, source_target_pairs={{8,0},{16,8},{24,16},{32,24},{40,32},{48,40},{56,48},{64,56},{72,6... | collective-permute-start | bytes 98312 | tf_op jit(solution)/shard_map/while/body/eval_jaxpr/ppermute | solution.py:12
  941.6 7.3 collective-permute-start.1
  990.1 7.1 collective-permute-start.1
  1029.5 146.5 %reduce-scatter.3.cloned.1.call-start = ((), (), s32[]{:S(2)}) async-start(), calls=%async_computation.2 | async-start | bytes 4718592 | tf_op jit(solution)/shard_map/reduce_scatter | solution.py:113
  (81 other events, 455.7 us)
Sparse Core Ops, SparseCore 0:
  1029.6 104.2 reduce-scatter.4
  1136.5 39.4 reduce-scatter.2
where the time goes:
time: 1200 us; the launch traced here: 1180 us
  waiting for transfers between devices  489 us (41%)
  starting transfers between devices  262 us (22%)
  local copies, waits for them, and re-layouts  136 us (11%)
  other arithmetic  115 us (10%)
  matrix products  112 us (9%)
  loops' own time  56.7 us (5%)
  between operations  14.1 us (1%)
    ppermute x78, waiting for transfers between devices, from_behind(): return lax.ppermute(value, axis, pairs)  350 us
    ppermute x78, starting transfers between devices, from_behind(): return lax.ppermute(value, axis, pairs)  262 us
    dynamic_update_slice x195, other arithmetic, store_slot(): return lax.dynamic_update_index_in_dim(buffer, chosen, slot_idx, 0)  111 us
    reduce_scatter x1, waiting for transfers between devices, per_device(): lax.psum_scatter(total_out.astype(jnp.bfloat16), 'dp', scatter_dimension=...  99.6 us
    dynamic_slice x78, local copies, waits for them, and re-layouts, per_device(): lax.scan(forward_tick, forward_init, jnp.arange(tick_count, dtype=jnp.int...  45.5 us
    broadcast_in_dim x62, local copies, waits for them, and re-layouts, per_device(): zero_hidden = jnp.zeros((row_count, hidden_dim), jnp.bfloat16)  44.8 us
    dynamic_slice x195, local copies, waits for them, and re-layouts, read_slot(): return lax.dynamic_index_in_dim(buffer, slot_idx, 0, keepdims=False)  40.2 us
    reduce_scatter x1, waiting for transfers between devices, per_device(): lax.psum_scatter(total_in.astype(jnp.bfloat16), 'dp', scatter_dimension=1...  39.9 us
  transfers between devices with their start and end apart: 80, of which 72 were waited for; matrix products, arithmetic and copies ran while one was open for 10% of the time, Pallas kernels for 0%

commit v1 on v0

v1 whole, which is shorter than its diff:
```python
import functools
import math

import jax
import jax.numpy as jnp
from jax import lax
from jax.experimental import pallas as pl
from jax.experimental.pallas import tpu as pltpu
from jax.sharding import PartitionSpec as P

WINDOW = 4
TILE = 512
VMEM_LIMIT = 12 * 1024 * 1024


def sigmoid(x):
    return 0.5 * jnp.tanh(0.5 * x) + 0.5


def forward_kernel(act_ref, win_ref, wout_ref, out_ref):
    act = act_ref[...]
    steps = win_ref.shape[1] // TILE

    def step(j, total):
        cols = pl.ds(pl.multiple_of(j * TILE, TILE), TILE)
        pre = jnp.dot(act, win_ref[:, cols], preferred_element_type=jnp.float32)
        hidden = (pre * sigmoid(pre)).astype(jnp.bfloat16)
        return total + jnp.dot(hidden, wout_ref[cols, :], preferred_element_type=jnp.float32)

    total = lax.fori_loop(0, steps, step, act.astype(jnp.float32), unroll=2)
    out_ref[...] = total.astype(jnp.bfloat16)


def backward_kernel(tick, sections, sec_ref, grad_ref, wout_t_ref, win_t_ref, slope_ref, out_ref):
    grad = grad_ref[...]
    steps = wout_t_ref.shape[1] // TILE
    slot = jnp.clip(tick - (sections - 1) + sec_ref[0], 0, slope_ref.shape[0] - 1)

    def step(j, total):
        cols = pl.ds(pl.multiple_of(j * TILE, TILE), TILE)
        through = jnp.dot(grad, wout_t_ref[:, cols], preferred_element_type=jnp.float32)
        grad_pre = (through * slope_ref[slot, :, cols]).astype(jnp.bfloat16)
        return total + jnp.dot(grad_pre, win_t_ref[cols, :], preferred_element_type=jnp.float32)

    total = lax.fori_loop(0, steps, step, grad.astype(jnp.float32), unroll=2)
    out_ref[...] = total.astype(jnp.bfloat16)


def slope_kernel(act_ref, win_ref, slope_ref):
    steps = win_ref.shape[1] // TILE

    def step(j, carry):
        cols = pl.ds(pl.multiple_of(j * TILE, TILE), TILE)
        for slot in range(act_ref.shape[0]):
            pre = jnp.dot(act_ref[slot], win_ref[:, cols], preferred_element_type=jnp.float32)
            sig = sigmoid(pre)
            slope_ref[slot, :, cols] = sig + pre * sig * (1.0 - sig)
        return carry

    lax.fori_loop(0, steps, step, 0)


def in_vmem():
    return pl.BlockSpec(memory_space=pltpu.VMEM)


def per_device(inputs, targets, w_in, w_out):
    sections = lax.axis_size("section")
    shares = lax.axis_size("dp")
    sec = lax.axis_index("section")
    share = lax.axis_index("dp")
    micro, rows, width = inputs.shape
    hidden_dim = w_in.shape[2]
    loss_scale = 1.0 / math.sqrt(micro * rows * shares)
    chunk = micro * rows // WINDOW
    inputs = inputs.reshape(WINDOW, chunk, width)
    targets = targets.reshape(WINDOW, chunk, width)
    weight_in, weight_out = w_in[0], w_out[0]
    is_first = sec == 0
    is_last = sec == sections - 1
    sec_arr = sec.astype(jnp.int32).reshape(1)
    params = pltpu.CompilerParams(vmem_limit_bytes=VMEM_LIMIT)
    rows_shape = jax.ShapeDtypeStruct((chunk, width), jnp.bfloat16)

    forward = pl.pallas_call(
        forward_kernel,
        out_shape=rows_shape,
        in_specs=[in_vmem()] * 3,
        out_specs=in_vmem(),
        compiler_params=params,
        name="fwd",
    )
    slope_of = pl.pallas_call(
        slope_kernel,
        out_shape=jax.ShapeDtypeStruct((WINDOW, chunk, hidden_dim), jnp.float32),
        in_specs=[in_vmem()] * 2,
        out_specs=in_vmem(),
        compiler_params=params,
        name="slope",
    )

    def backward(tick):
        return pl.pallas_call(
            functools.partial(backward_kernel, tick, sections),
            out_shape=rows_shape,
            in_specs=[pl.BlockSpec(memory_space=pltpu.SMEM)] + [in_vmem()] * 4,
            out_specs=in_vmem(),
            compiler_params=params,
            name="bwd",
        )

    ticks = sections + WINDOW - 1
    received = []
    tops = []
    act = jnp.where(is_first, inputs[0], jnp.zeros_like(inputs[0]))
    for tick in range(ticks):
        out = forward(act, weight_in, weight_out)
        if tick >= sections - 1:
            tops.append(out)
        if tick < ticks - 1:
            pairs = [(s, s + 1) for s in range(sections - 1) if 0 <= tick - s < WINDOW]
            act = lax.ppermute(out, "section", pairs)
            received.append(act)
            if tick + 1 < WINDOW:
                act = jnp.where(is_first, inputs[tick + 1], act)
    acts = jnp.where(
        is_first,
        inputs,
        lax.dynamic_slice_in_dim(jnp.stack(received), jnp.maximum(sec - 1, 0), WINDOW, 0),
    )
    slopes = slope_of(acts, weight_in)
    top_grad = (
        (jnp.stack(tops).astype(jnp.float32) - targets.astype(jnp.float32)) * loss_scale
    ).astype(jnp.bfloat16)

    weight_in_t, weight_out_t = weight_in.T, weight_out.T
    arrived = []
    grad = jnp.where(is_last, top_grad[0], jnp.zeros_like(top_grad[0]))
    for tick in range(ticks - 1):
        out = backward(tick)(sec_arr, grad, weight_out_t, weight_in_t, slopes)
        pairs = [(s, s - 1) for s in range(1, sections) if 0 <= tick - (sections - 1 - s) < WINDOW]
        grad = lax.ppermute(out, "section", pairs)
        arrived.append(grad)
        if tick + 1 < WINDOW:
            grad = jnp.where(is_last, top_grad[tick + 1], grad)
    start = jnp.maximum(sections - 2 - sec, 0)
    grads = jnp.where(
        is_last, top_grad, lax.dynamic_slice_in_dim(jnp.stack(arrived), start, WINDOW, 0)
    )

    all_acts = lax.all_gather(acts.reshape(micro * rows, width), "dp", tiled=True)
    all_grads = lax.all_gather(grads.reshape(micro * rows, width), "dp", tiled=True)
    part = hidden_dim // shares
    in_part = lax.dynamic_slice_in_dim(weight_in, share * part, part, 1)
    out_part = lax.dynamic_slice_in_dim(weight_out, share * part, part, 0)
    pre = jnp.dot(all_acts, in_part, preferred_element_type=jnp.float32)
    sig = sigmoid(pre)
    hidden = (pre * sig).astype(jnp.bfloat16)
    slope = sig + pre * sig * (1.0 - sig)
    through = jnp.einsum("rd,fd->rf", all_grads, out_part, preferred_element_type=jnp.float32)
    grad_pre = (through * slope).astype(jnp.bfloat16)
    share_in = jnp.einsum("rd,rf->df", all_acts, grad_pre, preferred_element_type=jnp.float32)
    share_out = jnp.einsum("rf,rd->fd", hidden, all_grads, preferred_element_type=jnp.float32)
    return (share_in[None], share_out[None])


def solution(mesh):
    in_specs = (
        P(None, "dp", None),
        P(None, "dp", None),
        P("section", None, None),
        P("section", None, None),
    )
    out_specs = (P("section", None, "dp"), P("section", "dp", None))
    return jax.shard_map(
        per_device, mesh=mesh, in_specs=in_specs, out_specs=out_specs, check_vma=False
    )
```

time: 1200 us -> 965 us (0.80); the launches traced: 1180 us -> 964 us
  waiting for transfers between devices: 489 us -> 103 us
  starting transfers between devices: 262 us -> 612 us
  Pallas kernels: 0 us -> 183 us
  other arithmetic: 115 us -> 1.98 us
  local copies, waits for them, and re-layouts: 136 us -> 30.9 us
  matrix products: 112 us -> 16.9 us
  loops' own time: 56.7 us -> 0 us
    ppermute x78 -> x68, starting transfers between devices: 262 us -> 612 us  [the longest x34 321 us: per_device(): act = lax.ppermute(out, 'section', pairs)]
    ppermute x78 -> x68, waiting for transfers between devices: 350 us -> 72 us  [the longest x34 68.1 us: per_device(): grad = lax.ppermute(out, 'section', pairs)]
    pallas_call x0 -> x70, Pallas kernels: none -> 183 us  [the longest x35 92.4 us: per_device(): out = forward(act, weight_in, weight_out)]
    reduce_scatter x2 -> x0, waiting for transfers between devices: 139 us -> none  [the longest x1 99.6 us: per_device(): lax.psum_scatter(total_out.astype(jnp.bfloat16), 'dp', scatter_dimension=...]
    dynamic_update_slice x195 -> x0, other arithmetic: 111 us -> none  [store_slot(): return lax.dynamic_update_index_in_dim(buffer, chosen, slot_idx, 0)]
    dot_general x42 -> x3, matrix products: 112 us -> 16.9 us  [the longest x1 6.76 us: per_device(): jnp.einsum('rd,rf->df', all_acts, grad_pre, preferred_element_type=jnp.fl...]
    dynamic_slice x273 -> x0, local copies, waits for them, and re-layouts: 85.7 us -> none  [the longest x78 45.5 us: per_device(): lax.scan(forward_tick, forward_init, jnp.arange(tick_count, dtype=jnp.int...]
    another operation x80 -> x0, loops' own time: 56.7 us -> none  [the longest x1 28 us: per_device(): lax.scan(forward_tick, forward_init, jnp.arange(tick_count, dtype=jnp.int...]
  transfers between devices with their start and end apart: 80 -> 70, of which waited for: 72 -> 8; matrix products, arithmetic and copies ran while one was open for 10% -> 2% of each run, Pallas kernels for 0% -> 9%
where the time goes in v1:
time: 965 us; the launch traced here: 964 us
  starting transfers between devices  612 us (63%)
  Pallas kernels  183 us (19%)
  waiting for transfers between devices  103 us (11%)
  local copies, waits for them, and re-layouts  30.9 us (3%)
  matrix products  16.9 us (2%)
  between operations  15.9 us (2%)
    ppermute x34, starting transfers between devices, per_device(): act = lax.ppermute(out, 'section', pairs)  321 us
    ppermute x34, starting transfers between devices, per_device(): grad = lax.ppermute(out, 'section', pairs)  291 us
    pallas_call x35, Pallas kernels, per_device(): out = forward(act, weight_in, weight_out)  92.4 us
    pallas_call x34, Pallas kernels, per_device(): out = backward(tick)(sec_arr, grad, weight_out_t, weight_in_t, slopes)  86.5 us
    ppermute x34, waiting for transfers between devices, per_device(): grad = lax.ppermute(out, 'section', pairs)  68.1 us
    unnamed x98, local copies, waits for them, and re-layouts  30.8 us
    all_gather x1, waiting for transfers between devices, per_device(): lax.all_gather(grads.reshape(micro * rows, width), 'dp', tiled=True)  30.8 us
  transfers between devices with their start and end apart: 70, of which 8 were waited for; matrix products, arithmetic and copies ran while one was open for 2% of the time, Pallas kernels for 9%

profile of v1, /device:TPU:1, one launch (start us, length us, event | category | flops | bytes accessed | tf_op | source)
XLA Modules:
  0.0 963.7 jit_solution(10053423087290785660)
XLA Ops:
  97.0 70.2 %collective-permute-start.15 = (bf16[64,512]{1,0:T(8,128)(2,1)S(1)}, bf16[64,512]{1,0:T(8,128)(2,1)S(1)}, u32[]{:S(2)}, u32[]{:S(2)}) collective-permute-start(bf16[64,512]{1,0:T(8,128)(2,1)S(1)} %fwd.50), channel_id=1, source_target_pairs={{96,104},{104,112},{112,120},{120,128},{97,105},{105,113},{113,121... | collective-permute-start | bytes 196616 | tf_op jit(solution)/shard_map/ppermute | solution.py:122
  237.4 15.8 %collective-permute-start.20 = (bf16[64,512]{1,0:T(8,128)(2,1)S(1)}, bf16[64,512]{1,0:T(8,128)(2,1)S(1)}, u32[]{:S(2)}, u32[]{:S(2)}) collective-permute-start(bf16[64,512]{1,0:T(8,128)(2,1)S(1)} %fwd.55), channel_id=1, source_target_pairs={{136,144},{144,152},{152,160},{160,168},{137,145},{145,153},{153,1... | collective-permute-start | bytes 196616 | tf_op jit(solution)/shard_map/ppermute | solution.py:122
  255.8 16.0 %collective-permute-start.21 = (bf16[64,512]{1,0:T(8,128)(2,1)S(1)}, bf16[64,512]{1,0:T(8,128)(2,1)S(1)}, u32[]{:S(2)}, u32[]{:S(2)}) collective-permute-start(bf16[64,512]{1,0:T(8,128)(2,1)S(1)} %fwd.56), channel_id=1, source_target_pairs={{144,152},{152,160},{160,168},{168,176},{145,153},{153,161},{161,1... | collective-permute-start | bytes 196616 | tf_op jit(solution)/shard_map/ppermute | solution.py:122
  274.5 16.0 %collective-permute-start.22 = (bf16[64,512]{1,0:T(8,128)(2,1)S(1)}, bf16[64,512]{1,0:T(8,128)(2,1)S(1)}, u32[]{:S(2)}, u32[]{:S(2)}) collective-permute-start(bf16[64,512]{1,0:T(8,128)(2,1)S(1)} %fwd.57), channel_id=1, source_target_pairs={{152,160},{160,168},{168,176},{176,184},{153,161},{161,169},{169,1... | collective-permute-start | bytes 196616 | tf_op jit(solution)/shard_map/ppermute | solution.py:122
  293.2 16.0 %collective-permute-start.23 = (bf16[64,512]{1,0:T(8,128)(2,1)S(1)}, bf16[64,512]{1,0:T(8,128)(2,1)S(1)}, u32[]{:S(2)}, u32[]{:S(2)}) collective-permute-start(bf16[64,512]{1,0:T(8,128)(2,1)S(1)} %fwd.58), channel_id=1, source_target_pairs={{160,168},{168,176},{176,184},{184,192},{161,169},{169,177},{177,1... | collective-permute-start | bytes 196616 | tf_op jit(solution)/shard_map/ppermute | solution.py:122
  311.9 16.0 %collective-permute-start.24 = (bf16[64,512]{1,0:T(8,128)(2,1)S(1)}, bf16[64,512]{1,0:T(8,128)(2,1)S(1)}, u32[]{:S(2)}, u32[]{:S(2)}) collective-permute-start(bf16[64,512]{1,0:T(8,128)(2,1)S(1)} %fwd.59), channel_id=1, source_target_pairs={{168,176},{176,184},{184,192},{192,200},{169,177},{177,185},{185,1... | collective-permute-start | bytes 196616 | tf_op jit(solution)/shard_map/ppermute | solution.py:122
  330.6 15.4 %collective-permute-start.25 = (bf16[64,512]{1,0:T(8,128)(2,1)S(1)}, bf16[64,512]{1,0:T(8,128)(2,1)S(1)}, u32[]{:S(2)}, u32[]{:S(2)}) collective-permute-start(bf16[64,512]{1,0:T(8,128)(2,1)S(1)} %fwd.60), channel_id=1, source_target_pairs={{176,184},{184,192},{192,200},{200,208},{177,185},{185,193},{193,2... | collective-permute-start | bytes 196616 | tf_op jit(solution)/shard_map/ppermute | solution.py:122
  382.9 15.5 %collective-permute-start.28 = (bf16[64,512]{1,0:T(8,128)(2,1)S(1)}, bf16[64,512]{1,0:T(8,128)(2,1)S(1)}, u32[]{:S(2)}, u32[]{:S(2)}) collective-permute-start(bf16[64,512]{1,0:T(8,128)(2,1)S(1)} %fwd.63), channel_id=1, source_target_pairs={{200,208},{208,216},{216,224},{224,232},{201,209},{209,217},{217,2... | collective-permute-start | bytes 196616 | tf_op jit(solution)/shard_map/ppermute | solution.py:122
  401.0 15.7 %collective-permute-start.29 = (bf16[64,512]{1,0:T(8,128)(2,1)S(1)}, bf16[64,512]{1,0:T(8,128)(2,1)S(1)}, u32[]{:S(2)}, u32[]{:S(2)}) collective-permute-start(bf16[64,512]{1,0:T(8,128)(2,1)S(1)} %fwd.64), channel_id=1, source_target_pairs={{208,216},{216,224},{224,232},{232,240},{209,217},{217,225},{225,2... | collective-permute-start | bytes 196616 | tf_op jit(solution)/shard_map/ppermute | solution.py:122
  419.4 15.7 %collective-permute-start.30 = (bf16[64,512]{1,0:T(8,128)(2,1)S(1)}, bf16[64,512]{1,0:T(8,128)(2,1)S(1)}, u32[]{:S(2)}, u32[]{:S(2)}) collective-permute-start(bf16[64,512]{1,0:T(8,128)(2,1)S(1)} %fwd.65), channel_id=1, source_target_pairs={{216,224},{224,232},{232,240},{240,248},{217,225},{225,233},{233,2... | collective-permute-start | bytes 196616 | tf_op jit(solution)/shard_map/ppermute | solution.py:122
  473.7 46.2 %collective-permute-start.37 = (bf16[64,512]{1,0:T(8,128)(2,1)S(1)}, bf16[64,512]{1,0:T(8,128)(2,1)S(1)}, u32[]{:S(2)}, u32[]{:S(2)}) collective-permute-start(bf16[64,512]{1,0:T(8,128)(2,1)S(1)} %bwd.37), channel_id=1, source_target_pairs={{224,216},{232,224},{240,232},{248,240},{225,217},{233,225},{241,2... | collective-permute-start | bytes 196616 | tf_op jit(solution)/shard_map/ppermute | solution.py:142
  522.5 16.0 %collective-permute-start.38 = (bf16[64,512]{1,0:T(8,128)(2,1)S(1)}, bf16[64,512]{1,0:T(8,128)(2,1)S(1)}, u32[]{:S(2)}, u32[]{:S(2)}) collective-permute-start(bf16[64,512]{1,0:T(8,128)(2,1)S(1)} %bwd.38), channel_id=1, source_target_pairs={{216,208},{224,216},{232,224},{240,232},{217,209},{225,217},{233,2... | collective-permute-start | bytes 196616 | tf_op jit(solution)/shard_map/ppermute | solution.py:142
  541.1 16.0 %collective-permute-start.39 = (bf16[64,512]{1,0:T(8,128)(2,1)S(1)}, bf16[64,512]{1,0:T(8,128)(2,1)S(1)}, u32[]{:S(2)}, u32[]{:S(2)}) collective-permute-start(bf16[64,512]{1,0:T(8,128)(2,1)S(1)} %bwd.39), channel_id=1, source_target_pairs={{208,200},{216,208},{224,216},{232,224},{209,201},{217,209},{225,2... | collective-permute-start | bytes 196616 | tf_op jit(solution)/shard_map/ppermute | solution.py:142
  559.6 16.0 %collective-permute-start.40 = (bf16[64,512]{1,0:T(8,128)(2,1)S(1)}, bf16[64,512]{1,0:T(8,128)(2,1)S(1)}, u32[]{:S(2)}, u32[]{:S(2)}) collective-permute-start(bf16[64,512]{1,0:T(8,128)(2,1)S(1)} %bwd.40), channel_id=1, source_target_pairs={{200,192},{208,200},{216,208},{224,216},{201,193},{209,201},{217,2... | collective-permute-start | bytes 196616 | tf_op jit(solution)/shard_map/ppermute | solution.py:142
  578.2 15.7 %collective-permute-start.41 = (bf16[64,512]{1,0:T(8,128)(2,1)S(1)}, bf16[64,512]{1,0:T(8,128)(2,1)S(1)}, u32[]{:S(2)}, u32[]{:S(2)}) collective-permute-start(bf16[64,512]{1,0:T(8,128)(2,1)S(1)} %bwd.41), channel_id=1, source_target_pairs={{192,184},{200,192},{208,200},{216,208},{193,185},{201,193},{209,2... | collective-permute-start | bytes 196616 | tf_op jit(solution)/shard_map/ppermute | solution.py:142
  612.5 15.0 %collective-permute-start.43 = (bf16[64,512]{1,0:T(8,128)(2,1)S(1)}, bf16[64,512]{1,0:T(8,128)(2,1)S(1)}, u32[]{:S(2)}, u32[]{:S(2)}) collective-permute-start(bf16[64,512]{1,0:T(8,128)(2,1)S(1)} %bwd.43), channel_id=1, source_target_pairs={{176,168},{184,176},{192,184},{200,192},{177,169},{185,177},{193,1... | collective-permute-start | bytes 196616 | tf_op jit(solution)/shard_map/ppermute | solution.py:142
  630.1 15.7 %collective-permute-start.44 = (bf16[64,512]{1,0:T(8,128)(2,1)S(1)}, bf16[64,512]{1,0:T(8,128)(2,1)S(1)}, u32[]{:S(2)}, u32[]{:S(2)}) collective-permute-start(bf16[64,512]{1,0:T(8,128)(2,1)S(1)} %bwd.44), channel_id=1, source_target_pairs={{168,160},{176,168},{184,176},{192,184},{169,161},{177,169},{185,1... | collective-permute-start | bytes 196616 | tf_op jit(solution)/shard_map/ppermute | solution.py:142
  648.3 16.3 %collective-permute-start.45 = (bf16[64,512]{1,0:T(8,128)(2,1)S(1)}, bf16[64,512]{1,0:T(8,128)(2,1)S(1)}, u32[]{:S(2)}, u32[]{:S(2)}) collective-permute-start(bf16[64,512]{1,0:T(8,128)(2,1)S(1)} %bwd.45), channel_id=1, source_target_pairs={{160,152},{168,160},{176,168},{184,176},{161,153},{169,161},{177,1... | collective-permute-start | bytes 196616 | tf_op jit(solution)/shard_map/ppermute | solution.py:142
  667.2 16.3 %collective-permute-start.46 = (bf16[64,512]{1,0:T(8,128)(2,1)S(1)}, bf16[64,512]{1,0:T(8,128)(2,1)S(1)}, u32[]{:S(2)}, u32[]{:S(2)}) collective-permute-start(bf16[64,512]{1,0:T(8,128)(2,1)S(1)} %bwd.46), channel_id=1, source_target_pairs={{152,144},{160,152},{168,160},{176,168},{153,145},{161,153},{169,1... | collective-permute-start | bytes 196616 | tf_op jit(solution)/shard_map/ppermute | solution.py:142
  686.0 16.3 %collective-permute-start.47 = (bf16[64,512]{1,0:T(8,128)(2,1)S(1)}, bf16[64,512]{1,0:T(8,128)(2,1)S(1)}, u32[]{:S(2)}, u32[]{:S(2)}) collective-permute-start(bf16[64,512]{1,0:T(8,128)(2,1)S(1)} %bwd.47), channel_id=1, source_target_pairs={{144,136},{152,144},{160,152},{168,160},{145,137},{153,145},{161,1... | collective-permute-start | bytes 196616 | tf_op jit(solution)/shard_map/ppermute | solution.py:142
  704.9 16.3 %collective-permute-start.48 = (bf16[64,512]{1,0:T(8,128)(2,1)S(1)}, bf16[64,512]{1,0:T(8,128)(2,1)S(1)}, u32[]{:S(2)}, u32[]{:S(2)}) collective-permute-start(bf16[64,512]{1,0:T(8,128)(2,1)S(1)} %bwd.48), channel_id=1, source_target_pairs={{136,128},{144,136},{152,144},{160,152},{137,129},{145,137},{153,1... | collective-permute-start | bytes 196616 | tf_op jit(solution)/shard_map/ppermute | solution.py:142
  723.8 16.0 %collective-permute-start.49 = (bf16[64,512]{1,0:T(8,128)(2,1)S(1)}, bf16[64,512]{1,0:T(8,128)(2,1)S(1)}, u32[]{:S(2)}, u32[]{:S(2)}) collective-permute-start(bf16[64,512]{1,0:T(8,128)(2,1)S(1)} %bwd.49), channel_id=1, source_target_pairs={{128,120},{136,128},{144,136},{152,144},{129,121},{137,129},{145,1... | collective-permute-start | bytes 196616 | tf_op jit(solution)/shard_map/ppermute | solution.py:142
  828.7 51.9 %collective-permute-done.64.grad_ref = bf16[64,512]{1,0:T(8,128)(2,1)S(1)} collective-permute-done((bf16[64,512]{1,0:T(8,128)(2,1)S(1)}, bf16[64,512]{1,0:T(8,128)(2,1)S(1)}, u32[]{:S(2)}, u32[]{:S(2)}) %collective-permute-start.64) | collective-permute-done | bytes 65568 | tf_op jit(solution)/shard_map/ppermute | solution.py:142
  914.1 30.8 %all-gather.5.cloned.1.call-done = bf16[2048,512]{1,0:T(8,128)(2,1)} async-done(((bf16[256,512]{1,0:T(8,128)(2,1)}), bf16[2048,512]{1,0:T(8,128)(2,1)}) %all-gather.5.cloned.1.call-update) | async-done | bytes 2097168 | tf_op jit(solution)/shard_map/all_gather | solution.py:152
  (302 shorter events, 430.7 us)
Async XLA Ops:
  7.2 902.0 %all-gather.3.cloned.1.call-start = ((), (), s32[]{:S(2)}) async-start(), calls=%async_computation | async-start | bytes 2359296 | tf_op jit(solution)/shard_map/all_gather | solution.py:151
  15.2 17.3 %collective-permute-start = (bf16[64,512]{1,0:T(8,128)(2,1)S(1)}, bf16[64,512]{1,0:T(8,128)(2,1)S(1)}, u32[]{:S(2)}, u32[]{:S(2)}) collective-permute-start(bf16[64,512]{1,0:T(8,128)(2,1)S(1)} %fwd.35), channel_id=1, source_target_pairs={{0,8},{1,9},{2,10},{3,11},{4,12},{5,13},{6,14},{7,15}} | collective-permute-start | bytes 196616 | tf_op jit(solution)/shard_map/ppermute | solution.py:122
  97.0 70.2 %collective-permute-start.15 = (bf16[64,512]{1,0:T(8,128)(2,1)S(1)}, bf16[64,512]{1,0:T(8,128)(2,1)S(1)}, u32[]{:S(2)}, u32[]{:S(2)}) collective-permute-start(bf16[64,512]{1,0:T(8,128)(2,1)S(1)} %fwd.50), channel_id=1, source_target_pairs={{96,104},{104,112},{112,120},{120,128},{97,105},{105,113},{113,121... | collective-permute-start | bytes 196616 | tf_op jit(solution)/shard_map/ppermute | solution.py:122
  237.4 15.8 %collective-permute-start.20 = (bf16[64,512]{1,0:T(8,128)(2,1)S(1)}, bf16[64,512]{1,0:T(8,128)(2,1)S(1)}, u32[]{:S(2)}, u32[]{:S(2)}) collective-permute-start(bf16[64,512]{1,0:T(8,128)(2,1)S(1)} %fwd.55), channel_id=1, source_target_pairs={{136,144},{144,152},{152,160},{160,168},{137,145},{145,153},{153,1... | collective-permute-start | bytes 196616 | tf_op jit(solution)/shard_map/ppermute | solution.py:122
  255.8 16.0 %collective-permute-start.21 = (bf16[64,512]{1,0:T(8,128)(2,1)S(1)}, bf16[64,512]{1,0:T(8,128)(2,1)S(1)}, u32[]{:S(2)}, u32[]{:S(2)}) collective-permute-start(bf16[64,512]{1,0:T(8,128)(2,1)S(1)} %fwd.56), channel_id=1, source_target_pairs={{144,152},{152,160},{160,168},{168,176},{145,153},{153,161},{161,1... | collective-permute-start | bytes 196616 | tf_op jit(solution)/shard_map/ppermute | solution.py:122
  274.5 16.0 %collective-permute-start.22 = (bf16[64,512]{1,0:T(8,128)(2,1)S(1)}, bf16[64,512]{1,0:T(8,128)(2,1)S(1)}, u32[]{:S(2)}, u32[]{:S(2)}) collective-permute-start(bf16[64,512]{1,0:T(8,128)(2,1)S(1)} %fwd.57), channel_id=1, source_target_pairs={{152,160},{160,168},{168,176},{176,184},{153,161},{161,169},{169,1... | collective-permute-start | bytes 196616 | tf_op jit(solution)/shard_map/ppermute | solution.py:122
  293.2 16.0 %collective-permute-start.23 = (bf16[64,512]{1,0:T(8,128)(2,1)S(1)}, bf16[64,512]{1,0:T(8,128)(2,1)S(1)}, u32[]{:S(2)}, u32[]{:S(2)}) collective-permute-start(bf16[64,512]{1,0:T(8,128)(2,1)S(1)} %fwd.58), channel_id=1, source_target_pairs={{160,168},{168,176},{176,184},{184,192},{161,169},{169,177},{177,1... | collective-permute-start | bytes 196616 | tf_op jit(solution)/shard_map/ppermute | solution.py:122
  311.9 16.0 %collective-permute-start.24 = (bf16[64,512]{1,0:T(8,128)(2,1)S(1)}, bf16[64,512]{1,0:T(8,128)(2,1)S(1)}, u32[]{:S(2)}, u32[]{:S(2)}) collective-permute-start(bf16[64,512]{1,0:T(8,128)(2,1)S(1)} %fwd.59), channel_id=1, source_target_pairs={{168,176},{176,184},{184,192},{192,200},{169,177},{177,185},{185,1... | collective-permute-start | bytes 196616 | tf_op jit(solution)/shard_map/ppermute | solution.py:122
  382.9 15.5 %collective-permute-start.28 = (bf16[64,512]{1,0:T(8,128)(2,1)S(1)}, bf16[64,512]{1,0:T(8,128)(2,1)S(1)}, u32[]{:S(2)}, u32[]{:S(2)}) collective-permute-start(bf16[64,512]{1,0:T(8,128)(2,1)S(1)} %fwd.63), channel_id=1, source_target_pairs={{200,208},{208,216},{216,224},{224,232},{201,209},{209,217},{217,2... | collective-permute-start | bytes 196616 | tf_op jit(solution)/shard_map/ppermute | solution.py:122
  401.0 15.8 %collective-permute-start.29 = (bf16[64,512]{1,0:T(8,128)(2,1)S(1)}, bf16[64,512]{1,0:T(8,128)(2,1)S(1)}, u32[]{:S(2)}, u32[]{:S(2)}) collective-permute-start(bf16[64,512]{1,0:T(8,128)(2,1)S(1)} %fwd.64), channel_id=1, source_target_pairs={{208,216},{216,224},{224,232},{232,240},{209,217},{217,225},{225,2... | collective-permute-start | bytes 196616 | tf_op jit(solution)/shard_map/ppermute | solution.py:122
  419.4 15.8 %collective-permute-start.30 = (bf16[64,512]{1,0:T(8,128)(2,1)S(1)}, bf16[64,512]{1,0:T(8,128)(2,1)S(1)}, u32[]{:S(2)}, u32[]{:S(2)}) collective-permute-start(bf16[64,512]{1,0:T(8,128)(2,1)S(1)} %fwd.65), channel_id=1, source_target_pairs={{216,224},{224,232},{232,240},{240,248},{217,225},{225,233},{233,2... | collective-permute-start | bytes 196616 | tf_op jit(solution)/shard_map/ppermute | solution.py:122
  457.9 487.0 %all-gather.5.cloned.1.call-start = ((), (), s32[]{:S(2)}) async-start(), calls=%async_computation.1 | async-start | bytes 2359296 | tf_op jit(solution)/shard_map/all_gather | solution.py:152
  473.7 46.3 %collective-permute-start.37 = (bf16[64,512]{1,0:T(8,128)(2,1)S(1)}, bf16[64,512]{1,0:T(8,128)(2,1)S(1)}, u32[]{:S(2)}, u32[]{:S(2)}) collective-permute-start(bf16[64,512]{1,0:T(8,128)(2,1)S(1)} %bwd.37), channel_id=1, source_target_pairs={{224,216},{232,224},{240,232},{248,240},{225,217},{233,225},{241,2... | collective-permute-start | bytes 196616 | tf_op jit(solution)/shard_map/ppermute | solution.py:142
  522.5 16.0 %collective-permute-start.38 = (bf16[64,512]{1,0:T(8,128)(2,1)S(1)}, bf16[64,512]{1,0:T(8,128)(2,1)S(1)}, u32[]{:S(2)}, u32[]{:S(2)}) collective-permute-start(bf16[64,512]{1,0:T(8,128)(2,1)S(1)} %bwd.38), channel_id=1, source_target_pairs={{216,208},{224,216},{232,224},{240,232},{217,209},{225,217},{233,2... | collective-permute-start | bytes 196616 | tf_op jit(solution)/shard_map/ppermute | solution.py:142
  541.1 16.0 %collective-permute-start.39 = (bf16[64,512]{1,0:T(8,128)(2,1)S(1)}, bf16[64,512]{1,0:T(8,128)(2,1)S(1)}, u32[]{:S(2)}, u32[]{:S(2)}) collective-permute-start(bf16[64,512]{1,0:T(8,128)(2,1)S(1)} %bwd.39), channel_id=1, source_target_pairs={{208,200},{216,208},{224,216},{232,224},{209,201},{217,209},{225,2... | collective-permute-start | bytes 196616 | tf_op jit(solution)/shard_map/ppermute | solution.py:142
  559.6 16.0 %collective-permute-start.40 = (bf16[64,512]{1,0:T(8,128)(2,1)S(1)}, bf16[64,512]{1,0:T(8,128)(2,1)S(1)}, u32[]{:S(2)}, u32[]{:S(2)}) collective-permute-start(bf16[64,512]{1,0:T(8,128)(2,1)S(1)} %bwd.40), channel_id=1, source_target_pairs={{200,192},{208,200},{216,208},{224,216},{201,193},{209,201},{217,2... | collective-permute-start | bytes 196616 | tf_op jit(solution)/shard_map/ppermute | solution.py:142
  578.2 15.8 %collective-permute-start.41 = (bf16[64,512]{1,0:T(8,128)(2,1)S(1)}, bf16[64,512]{1,0:T(8,128)(2,1)S(1)}, u32[]{:S(2)}, u32[]{:S(2)}) collective-permute-start(bf16[64,512]{1,0:T(8,128)(2,1)S(1)} %bwd.41), channel_id=1, source_target_pairs={{192,184},{200,192},{208,200},{216,208},{193,185},{201,193},{209,2... | collective-permute-start | bytes 196616 | tf_op jit(solution)/shard_map/ppermute | solution.py:142
  630.1 15.7 %collective-permute-start.44 = (bf16[64,512]{1,0:T(8,128)(2,1)S(1)}, bf16[64,512]{1,0:T(8,128)(2,1)S(1)}, u32[]{:S(2)}, u32[]{:S(2)}) collective-permute-start(bf16[64,512]{1,0:T(8,128)(2,1)S(1)} %bwd.44), channel_id=1, source_target_pairs={{168,160},{176,168},{184,176},{192,184},{169,161},{177,169},{185,1... | collective-permute-start | bytes 196616 | tf_op jit(solution)/shard_map/ppermute | solution.py:142
  648.3 16.3 %collective-permute-start.45 = (bf16[64,512]{1,0:T(8,128)(2,1)S(1)}, bf16[64,512]{1,0:T(8,128)(2,1)S(1)}, u32[]{:S(2)}, u32[]{:S(2)}) collective-permute-start(bf16[64,512]{1,0:T(8,128)(2,1)S(1)} %bwd.45), channel_id=1, source_target_pairs={{160,152},{168,160},{176,168},{184,176},{161,153},{169,161},{177,1... | collective-permute-start | bytes 196616 | tf_op jit(solution)/shard_map/ppermute | solution.py:142
  667.2 16.3 %collective-permute-start.46 = (bf16[64,512]{1,0:T(8,128)(2,1)S(1)}, bf16[64,512]{1,0:T(8,128)(2,1)S(1)}, u32[]{:S(2)}, u32[]{:S(2)}) collective-permute-start(bf16[64,512]{1,0:T(8,128)(2,1)S(1)} %bwd.46), channel_id=1, source_target_pairs={{152,144},{160,152},{168,160},{176,168},{153,145},{161,153},{169,1... | collective-permute-start | bytes 196616 | tf_op jit(solution)/shard_map/ppermute | solution.py:142
  686.0 16.3 %collective-permute-start.47 = (bf16[64,512]{1,0:T(8,128)(2,1)S(1)}, bf16[64,512]{1,0:T(8,128)(2,1)S(1)}, u32[]{:S(2)}, u32[]{:S(2)}) collective-permute-start(bf16[64,512]{1,0:T(8,128)(2,1)S(1)} %bwd.47), channel_id=1, source_target_pairs={{144,136},{152,144},{160,152},{168,160},{145,137},{153,145},{161,1... | collective-permute-start | bytes 196616 | tf_op jit(solution)/shard_map/ppermute | solution.py:142
  704.9 16.3 %collective-permute-start.48 = (bf16[64,512]{1,0:T(8,128)(2,1)S(1)}, bf16[64,512]{1,0:T(8,128)(2,1)S(1)}, u32[]{:S(2)}, u32[]{:S(2)}) collective-permute-start(bf16[64,512]{1,0:T(8,128)(2,1)S(1)} %bwd.48), channel_id=1, source_target_pairs={{136,128},{144,136},{152,144},{160,152},{137,129},{145,137},{153,1... | collective-permute-start | bytes 196616 | tf_op jit(solution)/shard_map/ppermute | solution.py:142
  723.8 16.0 %collective-permute-start.49 = (bf16[64,512]{1,0:T(8,128)(2,1)S(1)}, bf16[64,512]{1,0:T(8,128)(2,1)S(1)}, u32[]{:S(2)}, u32[]{:S(2)}) collective-permute-start(bf16[64,512]{1,0:T(8,128)(2,1)S(1)} %bwd.49), channel_id=1, source_target_pairs={{128,120},{136,128},{144,136},{152,144},{129,121},{137,129},{145,1... | collective-permute-start | bytes 196616 | tf_op jit(solution)/shard_map/ppermute | solution.py:142
  827.4 53.2 %collective-permute-start.64 = (bf16[64,512]{1,0:T(8,128)(2,1)S(1)}, bf16[64,512]{1,0:T(8,128)(2,1)S(1)}, u32[]{:S(2)}, u32[]{:S(2)}) collective-permute-start(bf16[64,512]{1,0:T(8,128)(2,1)S(1)} %bwd.64), channel_id=1, source_target_pairs={{8,0},{16,8},{24,16},{32,24},{9,1},{17,9},{25,17},{33,25},{10,2},{... | collective-permute-start | bytes 196616 | tf_op jit(solution)/shard_map/ppermute | solution.py:142
  (61 other events, 305.1 us)
Sparse Core Ops, SparseCore 0:
  458.0 49.3 all-gather.2
  909.2 35.6 all-gather.4

commit v2 on v1

v2 whole, which is shorter than its diff:
```python
import functools
import math

import jax
import jax.numpy as jnp
from jax import lax
from jax.experimental import pallas as pl
from jax.experimental.pallas import tpu as pltpu
from jax.sharding import PartitionSpec as P

WINDOW = 4
TILE = 1024
PARTS = 4
VMEM_LIMIT = 12 * 1024 * 1024


def sigmoid(x):
    return 0.5 * jnp.tanh(0.5 * x) + 0.5


def forward_kernel(act_ref, win_ref, wout_ref, out_ref):
    act = act_ref[...]
    total = act.astype(jnp.float32)
    for low in range(0, win_ref.shape[1], TILE):
        cols = slice(low, low + TILE)
        pre = jnp.dot(act, win_ref[:, cols], preferred_element_type=jnp.float32)
        hidden = (pre * sigmoid(pre)).astype(jnp.bfloat16)
        total = total + jnp.dot(hidden, wout_ref[cols, :], preferred_element_type=jnp.float32)
    out_ref[...] = total.astype(jnp.bfloat16)


def backward_kernel(tick, sections, sec_ref, grad_ref, slope_ref, *refs):
    weights, out_ref = refs[:-1], refs[-1]
    count = len(weights) // 2
    grad = grad_ref[...]
    total = grad.astype(jnp.float32)
    slot = jnp.clip(tick - (sections - 1) + sec_ref[0], 0, slope_ref.shape[0] - 1)
    part = weights[0].shape[1]
    for n in range(count):
        through = jnp.dot(grad, weights[n][...], preferred_element_type=jnp.float32)
        slope = slope_ref[slot, :, n * part : (n + 1) * part]
        grad_pre = (through * slope).astype(jnp.bfloat16)
        total = total + jnp.dot(
            grad_pre, weights[count + n][...], preferred_element_type=jnp.float32
        )
    out_ref[...] = total.astype(jnp.bfloat16)


def slope_kernel(act_ref, win_ref, slope_ref):
    slots, chunk, width = act_ref.shape
    act = act_ref[...].reshape(slots * chunk, width)
    steps = win_ref.shape[1] // 512

    def step(j, carry):
        cols = pl.ds(pl.multiple_of(j * 512, 512), 512)
        pre = jnp.dot(act, win_ref[:, cols], preferred_element_type=jnp.float32)
        sig = sigmoid(pre)
        slope = sig + pre * sig * (1.0 - sig)
        slope_ref[:, :, cols] = slope.reshape(slots, chunk, 512)
        return carry

    lax.fori_loop(0, steps, step, 0, unroll=2)


def turn_kernel(low, size, dim, after_ref, weight_ref, out_ref):
    if dim == 0:
        out_ref[...] = weight_ref[low : low + size, :].T
    else:
        out_ref[...] = weight_ref[:, low : low + size].T


def sending(tick):
    base = tick - tick % 2
    return range(base - WINDOW + 1, base + 2)


def in_vmem():
    return pl.BlockSpec(memory_space=pltpu.VMEM)


def per_device(inputs, targets, w_in, w_out):
    sections = lax.axis_size("section")
    shares = lax.axis_size("dp")
    sec = lax.axis_index("section")
    share = lax.axis_index("dp")
    micro, rows, width = inputs.shape
    hidden_dim = w_in.shape[2]
    loss_scale = 1.0 / math.sqrt(micro * rows * shares)
    chunk = micro * rows // WINDOW
    inputs = inputs.reshape(WINDOW, chunk, width)
    targets = targets.reshape(WINDOW, chunk, width)
    weight_in, weight_out = w_in[0], w_out[0]
    is_first = sec == 0
    is_last = sec == sections - 1
    sec_arr = sec.astype(jnp.int32).reshape(1)
    params = pltpu.CompilerParams(vmem_limit_bytes=VMEM_LIMIT)
    rows_shape = jax.ShapeDtypeStruct((chunk, width), jnp.bfloat16)

    forward = pl.pallas_call(
        forward_kernel,
        out_shape=rows_shape,
        in_specs=[in_vmem()] * 3,
        out_specs=in_vmem(),
        compiler_params=params,
        name="fwd",
    )
    slope_of = pl.pallas_call(
        slope_kernel,
        out_shape=jax.ShapeDtypeStruct((WINDOW, chunk, hidden_dim), jnp.float32),
        in_specs=[in_vmem()] * 2,
        out_specs=in_vmem(),
        compiler_params=params,
        name="slope",
    )

    def backward(tick):
        return pl.pallas_call(
            functools.partial(backward_kernel, tick, sections),
            out_shape=rows_shape,
            in_specs=[pl.BlockSpec(memory_space=pltpu.SMEM)] + [in_vmem()] * (2 + 2 * PARTS),
            out_specs=in_vmem(),
            compiler_params=params,
            name="bwd",
        )

    piece = hidden_dim // PARTS

    def turned_part(low, dim):
        shape = (width, piece) if dim == 0 else (piece, width)
        return pl.pallas_call(
            functools.partial(turn_kernel, low, piece, dim),
            out_shape=jax.ShapeDtypeStruct(shape, jnp.bfloat16),
            in_specs=[pl.BlockSpec(memory_space=pl.ANY), in_vmem()],
            out_specs=in_vmem(),
            compiler_params=params,
            name="turn",
        )

    ticks = sections + WINDOW - 1
    act_start = jnp.maximum(sec - 1, 0).astype(jnp.uint32)
    grad_start = jnp.maximum(sections - 2 - sec, 0).astype(jnp.uint32)
    part = hidden_dim // shares
    share_start = (share * part).astype(jnp.uint32)
    act = jnp.where(is_first, inputs[0], jnp.zeros_like(inputs[0]))
    act, sec_arr, act_start, grad_start, share_start, is_first, is_last = (
        lax.optimization_barrier(
            (act, sec_arr, act_start, grad_start, share_start, is_first, is_last)
        )
    )
    received = []
    tops = []
    turned = []
    for tick in range(ticks):
        out = forward(act, weight_in, weight_out)
        if tick >= sections - 1:
            tops.append(out)
        if tick < ticks - 1:
            pairs = [(s, s + 1) for s in sending(tick) if 0 <= s < sections - 1]
            act = lax.ppermute(out, "section", pairs)
            turn = tick - WINDOW
            if 0 <= turn < 2 * PARTS:
                low = turn % PARTS * piece
                if turn < PARTS:
                    block = turned_part(low, 0)(out, weight_out)
                else:
                    block = turned_part(low, 1)(out, weight_in)
                act, block = lax.optimization_barrier((act, block))
                turned.append(block)
            received.append(act)
            if tick + 1 < WINDOW:
                act = jnp.where(is_first, inputs[tick + 1], act)
    acts = jnp.where(
        is_first,
        inputs,
        lax.dynamic_slice_in_dim(jnp.stack(received), act_start, WINDOW, 0),
    )
    slopes = slope_of(acts, weight_in)
    top_grad = (
        (jnp.stack(tops).astype(jnp.float32) - targets.astype(jnp.float32)) * loss_scale
    ).astype(jnp.bfloat16)

    arrived = []
    grad = jnp.where(is_last, top_grad[0], jnp.zeros_like(top_grad[0]))
    for tick in range(ticks - 1):
        out = backward(tick)(sec_arr, grad, slopes, *turned)
        pairs = [(sections - 1 - k, sections - 2 - k) for k in sending(tick) if 0 <= k < sections - 1]
        grad = lax.ppermute(out, "section", pairs)
        arrived.append(grad)
        if tick + 1 < WINDOW:
            grad = jnp.where(is_last, top_grad[tick + 1], grad)

    in_part = lax.dynamic_slice_in_dim(weight_in, share_start, part, 1)
    out_part = lax.dynamic_slice_in_dim(weight_out, share_start, part, 0)
    grads = jnp.where(
        is_last,
        top_grad,
        lax.dynamic_slice_in_dim(jnp.stack(arrived), grad_start, WINDOW, 0),
    )
    all_acts = lax.all_gather(acts.reshape(micro * rows, width), "dp", tiled=True)
    all_grads = lax.all_gather(grads.reshape(micro * rows, width), "dp", tiled=True)
    pre = jnp.dot(all_acts, in_part, preferred_element_type=jnp.float32)
    sig = sigmoid(pre)
    hidden = (pre * sig).astype(jnp.bfloat16)
    slope = sig + pre * sig * (1.0 - sig)
    through = jnp.einsum("rd,fd->rf", all_grads, out_part, preferred_element_type=jnp.float32)
    grad_pre = (through * slope).astype(jnp.bfloat16)
    share_in = jnp.einsum("rd,rf->df", all_acts, grad_pre, preferred_element_type=jnp.float32)
    share_out = jnp.einsum("rf,rd->fd", hidden, all_grads, preferred_element_type=jnp.float32)
    return (share_in[None], share_out[None])


def solution(mesh):
    in_specs = (
        P(None, "dp", None),
        P(None, "dp", None),
        P("section", None, None),
        P("section", None, None),
    )
    out_specs = (P("section", None, "dp"), P("section", "dp", None))
    return jax.shard_map(
        per_device, mesh=mesh, in_specs=in_specs, out_specs=out_specs, check_vma=False
    )
```

time: 965 us -> 576 us (0.60)
  starting transfers between devices: 612 us -> 62.5 us
  waiting for transfers between devices: 103 us -> 335 us
  Pallas kernels: 183 us -> 116 us
  local copies, waits for them, and re-layouts: 30.9 us -> 15.2 us
    ppermute x34, starting transfers between devices: 321 us -> 36.2 us  [per_device(): act = lax.ppermute(out, 'section', pairs)]
    ppermute x34, starting transfers between devices: 291 us -> 26.2 us  [per_device(): grad = lax.ppermute(out, 'section', pairs)]
    ppermute x34, waiting for transfers between devices: 68.1 us -> 250 us  [per_device(): grad = lax.ppermute(out, 'section', pairs)]
    all_gather x1, waiting for transfers between devices: 30.8 us -> 79.5 us  [per_device(): lax.all_gather(grads.reshape(micro * rows, width), 'dp', tiled=True)]
    pallas_call x35, Pallas kernels: 92.4 us -> 57.4 us  [per_device(): out = forward(act, weight_in, weight_out)]
    pallas_call x34 -> x42, Pallas kernels: 86.5 us -> 56.8 us  [the longest x34 54.1 us: per_device(): out = backward(tick)(sec_arr, grad, slopes, *turned)]
    unnamed x98 -> x120, local copies, waits for them, and re-layouts: 30.8 us -> 15.2 us
  transfers between devices with their start and end apart: 70 -> 70, of which waited for: 8 -> 9; matrix products, arithmetic and copies ran while one was open for 2% -> 1% of each run, Pallas kernels for 9% -> 10%
where the time goes in v2:
time: 576 us; the launch traced here: 566 us
  waiting for transfers between devices  335 us (58%)
  Pallas kernels  116 us (20%)
  starting transfers between devices  62.5 us (11%)
  matrix products  17.1 us (3%)
  between operations  17 us (3%)
  local copies, waits for them, and re-layouts  15.2 us (3%)
    ppermute x34, waiting for transfers between devices, per_device(): grad = lax.ppermute(out, 'section', pairs)  250 us
    all_gather x1, waiting for transfers between devices, per_device(): lax.all_gather(grads.reshape(micro * rows, width), 'dp', tiled=True)  79.5 us
    pallas_call x35, Pallas kernels, per_device(): out = forward(act, weight_in, weight_out)  57.4 us
    pallas_call x34, Pallas kernels, per_device(): out = backward(tick)(sec_arr, grad, slopes, *turned)  54.1 us
    ppermute x34, starting transfers between devices, per_device(): act = lax.ppermute(out, 'section', pairs)  36.2 us
    ppermute x34, starting transfers between devices, per_device(): grad = lax.ppermute(out, 'section', pairs)  26.2 us
    unnamed x120, local copies, waits for them, and re-layouts  15.2 us
  transfers between devices with their start and end apart: 70, of which 9 were waited for; matrix products, arithmetic and copies ran while one was open for 1% of the time, Pallas kernels for 10%

profile of v2, /device:TPU:1, one launch (start us, length us, event | category | flops | bytes accessed | tf_op | source)
XLA Modules:
  0.0 566.2 jit_solution(8654243197532172213)
XLA Ops:
  8.2 2.2 copy-done
  10.4 2.2 copy-done.2
  14.2 4.4 collective-permute-start
  21.6 3.7 collective-permute-start.1
  28.2 3.7 collective-permute-start.2
  34.9 3.7 collective-permute-start.3
  42.6 1.8 copy-done.1
  66.1 1.6 fwd.48
  70.8 1.6 fwd.50
  75.5 1.6 fwd.52
  80.4 1.6 fwd.54
  85.1 1.6 fwd.56
  89.7 1.6 fwd.58
  104.0 1.6 fwd.64
  115.9 2.3 slope.1.slope_ref
  123.4 2.2 copy-done.5
  202.1 234.6 %collective-permute-done.64.grad_ref = bf16[64,512]{1,0:T(8,128)(2,1)S(1)} collective-permute-done((bf16[64,512]{1,0:T(8,128)(2,1)S(1)}, bf16[64,512]{1,0:T(8,128)(2,1)S(1)}, u32[]{:S(2)}, u32[]{:S(2)}) %collective-permute-start.64) | collective-permute-done | bytes 65568 | tf_op jit(solution)/shard_map/ppermute | solution.py:187
  439.9 5.6 collective-permute-done.65.grad_ref
  448.4 5.8 %collective-permute-done.66.grad_ref = bf16[64,512]{1,0:T(8,128)(2,1)S(1)} collective-permute-done((bf16[64,512]{1,0:T(8,128)(2,1)S(1)}, bf16[64,512]{1,0:T(8,128)(2,1)S(1)}, u32[]{:S(2)}, u32[]{:S(2)}) %collective-permute-start.66) | collective-permute-done | bytes 65568 | tf_op jit(solution)/shard_map/ppermute | solution.py:187
  457.1 4.3 collective-permute-done.67
  462.3 5.1 fusion.10
  467.4 79.5 %all-gather.5.cloned.1.call-done = bf16[2048,512]{1,0:T(8,128)(2,1)} async-done(((bf16[256,512]{1,0:T(8,128)(2,1)}), bf16[2048,512]{1,0:T(8,128)(2,1)}) %all-gather.5.cloned.1.call-update) | async-done | bytes 2097168 | tf_op jit(solution)/shard_map/all_gather | solution.py:200
  546.9 5.1 fusion.5
  552.1 6.8 %convolution_bitcast_fusion = f32[1,512,512]{2,1,0:T(8,128)} fusion(bf16[2048,512]{1,0:T(8,128)(2,1)S(1)} %copy-done.21, f32[2048,512]{1,0:T(8,128)} %fusion.10, bf16[2048,512]{1,0:T(8,128)(2,1)} %all-gather.5.cloned.1.call-done, bf16[1,4096,512]{2,1,0:T(8,128)(2,1)} %param.7, u32[]{:T(128)S(6)} %convert_element_type.29), kind=kOutput, calls=%fused_computation.7 | convolution fusion | flops 2156920832 | bytes 9961476 | tf_op jit(solution)/shard_map/rd,rf->df/dot_general | solution.py:207
  (332 shorter events, 164.8 us)
Async XLA Ops:
  7.2 455.1 %all-gather.3.cloned.1.call-start = ((), (), s32[]{:S(2)}) async-start(), calls=%async_computation | async-start | bytes 2359296 | tf_op jit(solution)/shard_map/all_gather | solution.py:199
  14.2 5.7 %collective-permute-start = (bf16[64,512]{1,0:T(8,128)(2,1)S(1)}, bf16[64,512]{1,0:T(8,128)(2,1)S(1)}, u32[]{:S(2)}, u32[]{:S(2)}) collective-permute-start(bf16[64,512]{1,0:T(8,128)(2,1)S(1)} %fwd.35), channel_id=1, source_target_pairs={{0,8},{8,16},{1,9},{9,17},{2,10},{10,18},{3,11},{11,19},{4,12},{12... | collective-permute-start | bytes 196616 | tf_op jit(solution)/shard_map/ppermute | solution.py:159
  21.6 5.0 collective-permute-start.1
  28.2 5.0 collective-permute-start.2
  34.9 5.0 collective-permute-start.3
  41.6 1.1 collective-permute-start.4
  46.1 1.0 collective-permute-start.5
  48.8 1.0 collective-permute-start.6
  51.5 1.1 collective-permute-start.7
  54.2 1.5 collective-permute-start.8
  57.4 1.0 collective-permute-start.9
  60.0 1.0 collective-permute-start.10
  62.7 1.0 collective-permute-start.11
  77.1 0.9 collective-permute-start.17
  100.8 0.9 collective-permute-start.27
  121.8 0.7 collective-permute-start.34
  122.5 424.4 %all-gather.5.cloned.1.call-start = ((), (), s32[]{:S(2)}) async-start(), calls=%async_computation.1 | async-start | bytes 2359296 | tf_op jit(solution)/shard_map/all_gather | solution.py:200
  133.3 1.1 collective-permute-start.35
  156.7 0.9 collective-permute-start.45
  179.9 0.9 collective-permute-start.55
  200.8 236.0 %collective-permute-start.64 = (bf16[64,512]{1,0:T(8,128)(2,1)S(1)}, bf16[64,512]{1,0:T(8,128)(2,1)S(1)}, u32[]{:S(2)}, u32[]{:S(2)}) collective-permute-start(bf16[64,512]{1,0:T(8,128)(2,1)S(1)} %bwd.64), channel_id=1, source_target_pairs={{32,24},{24,16},{16,8},{8,0},{33,25},{25,17},{17,9},{9,1},{34,26},... | collective-permute-start | bytes 196616 | tf_op jit(solution)/shard_map/ppermute | solution.py:187
  438.4 7.1 %collective-permute-start.65 = (bf16[64,512]{1,0:T(8,128)(2,1)S(1)}, bf16[64,512]{1,0:T(8,128)(2,1)S(1)}, u32[]{:S(2)}, u32[]{:S(2)}) collective-permute-start(bf16[64,512]{1,0:T(8,128)(2,1)S(1)} %bwd.65), channel_id=1, source_target_pairs={{32,24},{24,16},{16,8},{8,0},{33,25},{25,17},{17,9},{9,1},{34,26},... | collective-permute-start | bytes 196616 | tf_op jit(solution)/shard_map/ppermute | solution.py:187
  447.1 7.1 %collective-permute-start.66 = (bf16[64,512]{1,0:T(8,128)(2,1)S(1)}, bf16[64,512]{1,0:T(8,128)(2,1)S(1)}, u32[]{:S(2)}, u32[]{:S(2)}) collective-permute-start(bf16[64,512]{1,0:T(8,128)(2,1)S(1)} %bwd.66), channel_id=1, source_target_pairs={{16,8},{8,0},{17,9},{9,1},{18,10},{10,2},{19,11},{11,3},{20,12},{1... | collective-permute-start | bytes 196616 | tf_op jit(solution)/shard_map/ppermute | solution.py:187
  455.8 5.6 collective-permute-start.67
  (73 other events, 502.2 us)
Sparse Core Ops, SparseCore 0:
  122.6 175.2 all-gather.2
  462.4 84.4 all-gather.4

commit v3 on v2

--- a/solution.py
+++ b/solution.py
@@ -8,7 +8,10 @@
 from jax.experimental.pallas import tpu as pltpu
 from jax.sharding import PartitionSpec as P
 
-WINDOW = 4
+STREAMS = 2
+ROUNDS = 2
+SHARED = 4
+WINDOW = STREAMS * ROUNDS
 TILE = 1024
 PARTS = 4
 VMEM_LIMIT = 12 * 1024 * 1024
@@ -29,12 +32,13 @@
     out_ref[...] = total.astype(jnp.bfloat16)
 
 
-def backward_kernel(tick, sections, sec_ref, grad_ref, slope_ref, *refs):
+def backward_kernel(tick, stream, sections, sec_ref, grad_ref, slope_ref, *refs):
     weights, out_ref = refs[:-1], refs[-1]
     count = len(weights) // 2
     grad = grad_ref[...]
     total = grad.astype(jnp.float32)
-    slot = jnp.clip(tick - (sections - 1) + sec_ref[0], 0, slope_ref.shape[0] - 1)
+    turn = jnp.clip(tick - (sections - 1) + sec_ref[0], 0, ROUNDS - 1)
+    slot = turn * STREAMS + stream
     part = weights[0].shape[1]
     for n in range(count):
         through = jnp.dot(grad, weights[n][...], preferred_element_type=jnp.float32)
@@ -70,8 +74,8 @@
 
 
 def sending(tick):
-    base = tick - tick % 2
-    return range(base - WINDOW + 1, base + 2)
+    base = tick - tick % SHARED
+    return range(base - ROUNDS + 1, base + SHARED)
 
 
 def in_vmem():
@@ -113,9 +117,9 @@
         name="slope",
     )
 
-    def backward(tick):
+    def backward(tick, stream):
         return pl.pallas_call(
-            functools.partial(backward_kernel, tick, sections),
+            functools.partial(backward_kernel, tick, stream, sections),
             out_shape=rows_shape,
             in_specs=[pl.BlockSpec(memory_space=pltpu.SMEM)] + [in_vmem()] * (2 + 2 * PARTS),
             out_specs=in_vmem(),
@@ -136,68 +140,73 @@
             name="turn",
         )
 
-    ticks = sections + WINDOW - 1
+    ticks = sections + ROUNDS - 1
+    streams = range(STREAMS)
     act_start = jnp.maximum(sec - 1, 0).astype(jnp.uint32)
     grad_start = jnp.maximum(sections - 2 - sec, 0).astype(jnp.uint32)
     part = hidden_dim // shares
     share_start = (share * part).astype(jnp.uint32)
-    act = jnp.where(is_first, inputs[0], jnp.zeros_like(inputs[0]))
+    act = [jnp.where(is_first, inputs[n], jnp.zeros_like(inputs[n])) for n in streams]
     act, sec_arr, act_start, grad_start, share_start, is_first, is_last = (
         lax.optimization_barrier(
             (act, sec_arr, act_start, grad_start, share_start, is_first, is_last)
         )
     )
-    received = []
+    received = [[] for _ in streams]
     tops = []
     turned = []
     for tick in range(ticks):
-        out = forward(act, weight_in, weight_out)
-        if tick >= sections - 1:
-            tops.append(out)
-        if tick < ticks - 1:
-            pairs = [(s, s + 1) for s in sending(tick) if 0 <= s < sections - 1]
-            act = lax.ppermute(out, "section", pairs)
-            turn = tick - WINDOW
-            if 0 <= turn < 2 * PARTS:
-                low = turn % PARTS * piece
-                if turn < PARTS:
-                    block = turned_part(low, 0)(out, weight_out)
-                else:
-                    block = turned_part(low, 1)(out, weight_in)
-                act, block = lax.optimization_barrier((act, block))
-                turned.append(block)
-            received.append(act)
-            if tick + 1 < WINDOW:
-                act = jnp.where(is_first, inputs[tick + 1], act)
-    acts = jnp.where(
-        is_first,
-        inputs,
-        lax.dynamic_slice_in_dim(jnp.stack(received), act_start, WINDOW, 0),
-    )
+        for n in streams:
+            out = forward(act[n], weight_in, weight_out)
+            if tick >= sections - 1:
+                tops.append(out)
+            if tick < ticks - 1:
+                pairs = [(s, s + 1) for s in sending(tick) if 0 <= s < sections - 1]
+                act[n] = lax.ppermute(out, "section", pairs)
+                turn = tick - ROUNDS
+                if n == 0 and 0 <= turn < 2 * PARTS:
+                    low = turn % PARTS * piece
+                    if turn < PARTS:
+                        block = turned_part(low, 0)(out, weight_out)
+                    else:
+                        block = turned_part(low, 1)(out, weight_in)
+                    act[n], block = lax.optimization_barrier((act[n], block))
+                    turned.append(block)
+                received[n].append(act[n])
+                if tick + 1 < ROUNDS:
+                    act[n] = jnp.where(is_first, inputs[(tick + 1) * STREAMS + n], act[n])
+
+    def picked(buffers, start, low, count):
+        slices = [
+            lax.dynamic_slice_in_dim(jnp.stack(buffers[n]), start + low, count, 0)
+            for n in streams
+        ]
+        return jnp.stack(slices, 1).reshape(count * STREAMS, chunk, width)
+
+    acts = jnp.where(is_first, inputs, picked(received, act_start, jnp.uint32(0), ROUNDS))
     slopes = slope_of(acts, weight_in)
     top_grad = (
         (jnp.stack(tops).astype(jnp.float32) - targets.astype(jnp.float32)) * loss_scale
     ).astype(jnp.bfloat16)
 
-    arrived = []
-    grad = jnp.where(is_last, top_grad[0], jnp.zeros_like(top_grad[0]))
+    arrived = [[] for _ in streams]
+    grad = [jnp.where(is_last, top_grad[n], jnp.zeros_like(top_grad[n])) for n in streams]
     for tick in range(ticks - 1):
-        out = backward(tick)(sec_arr, grad, slopes, *turned)
-        pairs = [(sections - 1 - k, sections - 2 - k) for k in sending(tick) if 0 <= k < sections - 1]
-        grad = lax.ppermute(out, "section", pairs)
-        arrived.append(grad)
-        if tick + 1 < WINDOW:
-            grad = jnp.where(is_last, top_grad[tick + 1], grad)
+        pairs = [
+            (sections - 1 - k, sections - 2 - k) for k in sending(tick) if 0 <= k < sections - 1
+        ]
+        for n in streams:
+            out = backward(tick, n)(sec_arr, grad[n], slopes, *turned)
+            grad[n] = lax.ppermute(out, "section", pairs)
+            arrived[n].append(grad[n])
+            if tick + 1 < ROUNDS:
+                grad[n] = jnp.where(is_last, top_grad[(tick + 1) * STREAMS + n], grad[n])
 
     in_part = lax.dynamic_slice_in_dim(weight_in, share_start, part, 1)
     out_part = lax.dynamic_slice_in_dim(weight_out, share_start, part, 0)
-    grads = jnp.where(
-        is_last,
-        top_grad,
-        lax.dynamic_slice_in_dim(jnp.stack(arrived), grad_start, WINDOW, 0),
-    )
-    all_acts = lax.all_gather(acts.reshape(micro * rows, width), "dp", tiled=True)
-    all_grads = lax.all_gather(grads.reshape(micro * rows, width), "dp", tiled=True)
+    grads = jnp.where(is_last, top_grad, picked(arrived, grad_start, jnp.uint32(0), ROUNDS))
+    all_acts = lax.all_gather(acts.reshape(-1, width), "dp", tiled=True)
+    all_grads = lax.all_gather(grads.reshape(-1, width), "dp", tiled=True)
     pre = jnp.dot(all_acts, in_part, preferred_element_type=jnp.float32)
     sig = sigmoid(pre)
     hidden = (pre * sig).astype(jnp.bfloat16)

time: 576 us -> 578 us (level)
  waiting for transfers between devices: 335 us -> 184 us
  Pallas kernels: 116 us -> 215 us
  starting transfers between devices: 62.5 us -> 113 us
    ppermute x68 -> x128, waiting for transfers between devices: 256 us -> 100 us  [the longest x64 99.8 us: per_device(): grad[n] = lax.ppermute(out, 'section', pairs)]
    pallas_call x69 -> x130, Pallas kernels: 112 us -> 210 us  [the longest x66 108 us: per_device(): out = forward(act[n], weight_in, weight_out)]
    ppermute x68 -> x128, starting transfers between devices: 62.4 us -> 113 us  [the longest x64 63.7 us: per_device(): act[n] = lax.ppermute(out, 'section', pairs)]
    unnamed x120 -> x178, local copies, waits for them, and re-layouts: 15.2 us -> 14.6 us
  transfers between devices with their start and end apart: 70 -> 130, of which waited for: 9 -> 9; matrix products, arithmetic and copies ran while one was open for 1% -> 2% of each run, Pallas kernels for 10% -> 38%
where the time goes in v3:
time: 578 us; the launch traced here: 568 us
  Pallas kernels  215 us (37%)
  waiting for transfers between devices  184 us (32%)
  starting transfers between devices  113 us (20%)
  between operations  18.8 us (3%)
  matrix products  17.1 us (3%)
  local copies, waits for them, and re-layouts  14.7 us (3%)
    pallas_call x66, Pallas kernels, per_device(): out = forward(act[n], weight_in, weight_out)  108 us
    pallas_call x64, Pallas kernels, per_device(): out = backward(tick, n)(sec_arr, grad[n], slopes, *turned)  102 us
    ppermute x64, waiting for transfers between devices, per_device(): grad[n] = lax.ppermute(out, 'section', pairs)  99.8 us
    all_gather x1, waiting for transfers between devices, per_device(): all_grads = lax.all_gather(grads.reshape(-1, width), 'dp', tiled=True)  83.6 us
    ppermute x64, starting transfers between devices, per_device(): act[n] = lax.ppermute(out, 'section', pairs)  63.7 us
    ppermute x64, starting transfers between devices, per_device(): grad[n] = lax.ppermute(out, 'section', pairs)  49.1 us
    unnamed x178, local copies, waits for them, and re-layouts  14.6 us
  transfers between devices with their start and end apart: 130, of which 9 were waited for; matrix products, arithmetic and copies ran while one was open for 2% of the time, Pallas kernels for 38%

profile of v3, /device:TPU:1, one launch (start us, length us, event | category | flops | bytes accessed | tf_op | source)
XLA Modules:
  0.0 568.2 jit_solution(9362725921859921493)
XLA Ops:
  8.2 2.2 copy-done
  10.4 2.2 copy-done.3
  14.2 4.5 collective-permute-start.32
  20.4 3.5 collective-permute-start
  26.4 3.5 collective-permute-start.33
  31.7 4.8 collective-permute-start.1
  38.1 1.9 collective-permute-start.34
  41.7 1.9 collective-permute-start.2
  44.1 1.8 copy-done.1
  47.5 1.9 collective-permute-start.35
  51.1 2.6 collective-permute-start.3
  67.9 1.6 fwd.72.after_ref
  70.6 2.2 copy-done.4
  95.1 1.6 fwd.77
  196.2 2.2 copy-done.2
  198.4 2.3 slope.1.slope_ref
  202.4 1.6 fwd.130
  356.4 91.0 %collective-permute-done.126.grad_ref = bf16[64,512]{1,0:T(8,128)(2,1)S(1)} collective-permute-done((bf16[64,512]{1,0:T(8,128)(2,1)S(1)}, bf16[64,512]{1,0:T(8,128)(2,1)S(1)}, u32[]{:S(2)}, u32[]{:S(2)}) %collective-permute-start.126) | collective-permute-done | bytes 65568 | tf_op jit(solution)/shard_map/ppermute | solution.py:200
  453.9 1.8 collective-permute-done.127
  455.7 3.5 collective-permute-done.95
  460.2 5.2 fusion.8
  465.5 83.6 %all-gather.5.cloned.1.call-done = bf16[2048,512]{1,0:T(8,128)(2,1)} async-done(((bf16[256,512]{1,0:T(8,128)(2,1)}), bf16[2048,512]{1,0:T(8,128)(2,1)}) %all-gather.5.cloned.1.call-update) | async-done | bytes 2097168 | tf_op jit(solution)/shard_map/all_gather | solution.py:209
  549.1 6.8 %convolution_bitcast_fusion = f32[1,512,512]{2,1,0:T(8,128)} fusion(bf16[2048,512]{1,0:T(8,128)(2,1)S(1)} %copy-done.20, f32[2048,512]{1,0:T(8,128)} %fusion.8, bf16[2048,512]{1,0:T(8,128)(2,1)} %all-gather.5.cloned.1.call-done, bf16[1,4096,512]{2,1,0:T(8,128)(2,1)} %param.7, u32[]{:T(128)S(6)} %convert_element_type.44), kind=kOutput, calls=%fused_computation.7 | convolution fusion | flops 2156920832 | bytes 9961476 | tf_op jit(solution)/shard_map/rd,rf->df/dot_general | solution.py:216
  555.8 5.1 fusion.5
  (579 shorter events, 309.9 us)
Async XLA Ops:
  7.2 453.0 %all-gather.3.cloned.1.call-start = ((), (), s32[]{:S(2)}) async-start(), calls=%async_computation | async-start | bytes 2359296 | tf_op jit(solution)/shard_map/all_gather | solution.py:208
  14.2 10.6 %collective-permute-start.32 = (bf16[64,512]{1,0:T(8,128)(2,1)S(1)}, bf16[64,512]{1,0:T(8,128)(2,1)S(1)}, u32[]{:S(2)}, u32[]{:S(2)}) collective-permute-start(bf16[64,512]{1,0:T(8,128)(2,1)S(1)} %fwd.98), channel_id=1, source_target_pairs={{0,8},{8,16},{16,24},{24,32},{1,9},{9,17},{17,25},{25,33},{2,10},{... | collective-permute-start | bytes 196616 | tf_op jit(solution)/shard_map/ppermute | solution.py:165
  20.4 9.6 %collective-permute-start = (bf16[64,512]{1,0:T(8,128)(2,1)S(1)}, bf16[64,512]{1,0:T(8,128)(2,1)S(1)}, u32[]{:S(2)}, u32[]{:S(2)}) collective-permute-start(bf16[64,512]{1,0:T(8,128)(2,1)S(1)} %fwd.66), channel_id=1, source_target_pairs={{0,8},{8,16},{16,24},{24,32},{1,9},{9,17},{17,25},{25,33},{2,10},{... | collective-permute-start | bytes 196616 | tf_op jit(solution)/shard_map/ppermute | solution.py:165
  26.4 10.0 %collective-permute-start.33 = (bf16[64,512]{1,0:T(8,128)(2,1)S(1)}, bf16[64,512]{1,0:T(8,128)(2,1)S(1)}, u32[]{:S(2)}, u32[]{:S(2)}) collective-permute-start(bf16[64,512]{1,0:T(8,128)(2,1)S(1)} %fwd.99), channel_id=1, source_target_pairs={{0,8},{8,16},{16,24},{24,32},{1,9},{9,17},{17,25},{25,33},{2,10},{... | collective-permute-start | bytes 196616 | tf_op jit(solution)/shard_map/ppermute | solution.py:165
  31.7 8.4 %collective-permute-start.1 = (bf16[64,512]{1,0:T(8,128)(2,1)S(1)}, bf16[64,512]{1,0:T(8,128)(2,1)S(1)}, u32[]{:S(2)}, u32[]{:S(2)}) collective-permute-start(bf16[64,512]{1,0:T(8,128)(2,1)S(1)} %fwd.67), channel_id=1, source_target_pairs={{0,8},{8,16},{16,24},{24,32},{1,9},{9,17},{17,25},{25,33},{2,10},{... | collective-permute-start | bytes 196616 | tf_op jit(solution)/shard_map/ppermute | solution.py:165
  38.1 5.9 %collective-permute-start.34 = (bf16[64,512]{1,0:T(8,128)(2,1)S(1)}, bf16[64,512]{1,0:T(8,128)(2,1)S(1)}, u32[]{:S(2)}, u32[]{:S(2)}) collective-permute-start(bf16[64,512]{1,0:T(8,128)(2,1)S(1)} %fwd.100), channel_id=1, source_target_pairs={{0,8},{8,16},{16,24},{24,32},{1,9},{9,17},{17,25},{25,33},{2,10},{... | collective-permute-start | bytes 196616 | tf_op jit(solution)/shard_map/ppermute | solution.py:165
  41.7 7.7 %collective-permute-start.2 = (bf16[64,512]{1,0:T(8,128)(2,1)S(1)}, bf16[64,512]{1,0:T(8,128)(2,1)S(1)}, u32[]{:S(2)}, u32[]{:S(2)}) collective-permute-start(bf16[64,512]{1,0:T(8,128)(2,1)S(1)} %fwd.68.after_ref), channel_id=1, source_target_pairs={{0,8},{8,16},{16,24},{24,32},{1,9},{9,17},{17,25},{25,33},{2,10},{... | collective-permute-start | bytes 196616 | tf_op jit(solution)/shard_map/ppermute | solution.py:165
  47.5 6.5 %collective-permute-start.35 = (bf16[64,512]{1,0:T(8,128)(2,1)S(1)}, bf16[64,512]{1,0:T(8,128)(2,1)S(1)}, u32[]{:S(2)}, u32[]{:S(2)}) collective-permute-start(bf16[64,512]{1,0:T(8,128)(2,1)S(1)} %fwd.101), channel_id=1, source_target_pairs={{0,8},{8,16},{16,24},{24,32},{1,9},{9,17},{17,25},{25,33},{2,10},{... | collective-permute-start | bytes 196616 | tf_op jit(solution)/shard_map/ppermute | solution.py:165
  51.1 5.7 %collective-permute-start.3 = (bf16[64,512]{1,0:T(8,128)(2,1)S(1)}, bf16[64,512]{1,0:T(8,128)(2,1)S(1)}, u32[]{:S(2)}, u32[]{:S(2)}) collective-permute-start(bf16[64,512]{1,0:T(8,128)(2,1)S(1)} %fwd.69.after_ref), channel_id=1, source_target_pairs={{0,8},{8,16},{16,24},{24,32},{1,9},{9,17},{17,25},{25,33},{2,10},{... | collective-permute-start | bytes 196616 | tf_op jit(solution)/shard_map/ppermute | solution.py:165
  55.7 3.8 collective-permute-start.36
  61.2 4.4 collective-permute-start.37
  63.5 4.3 collective-permute-start.5
  69.5 5.6 collective-permute-start.6
  81.8 3.6 collective-permute-start.8
  195.7 353.3 %all-gather.5.cloned.1.call-start = ((), (), s32[]{:S(2)}) async-start(), calls=%async_computation.1 | async-start | bytes 2359296 | tf_op jit(solution)/shard_map/all_gather | solution.py:209
  335.1 3.6 collective-permute-start.91
  337.5 5.0 collective-permute-start.124
  340.4 5.6 collective-permute-start.92
  344.1 6.2 %collective-permute-start.125 = (bf16[64,512]{1,0:T(8,128)(2,1)S(1)}, bf16[64,512]{1,0:T(8,128)(2,1)S(1)}, u32[]{:S(2)}, u32[]{:S(2)}) collective-permute-start(bf16[64,512]{1,0:T(8,128)(2,1)S(1)} %bwd.125), channel_id=1, source_target_pairs={{32,24},{24,16},{16,8},{8,0},{33,25},{25,17},{17,9},{9,1},{34,26},... | collective-permute-start | bytes 196616 | tf_op jit(solution)/shard_map/ppermute | solution.py:200
  347.6 5.9 %collective-permute-start.93 = (bf16[64,512]{1,0:T(8,128)(2,1)S(1)}, bf16[64,512]{1,0:T(8,128)(2,1)S(1)}, u32[]{:S(2)}, u32[]{:S(2)}) collective-permute-start(bf16[64,512]{1,0:T(8,128)(2,1)S(1)} %bwd.93), channel_id=1, source_target_pairs={{32,24},{24,16},{16,8},{8,0},{33,25},{25,17},{17,9},{9,1},{34,26},... | collective-permute-start | bytes 196616 | tf_op jit(solution)/shard_map/ppermute | solution.py:200
  351.8 95.6 %collective-permute-start.126 = (bf16[64,512]{1,0:T(8,128)(2,1)S(1)}, bf16[64,512]{1,0:T(8,128)(2,1)S(1)}, u32[]{:S(2)}, u32[]{:S(2)}) collective-permute-start(bf16[64,512]{1,0:T(8,128)(2,1)S(1)} %bwd.126), channel_id=1, source_target_pairs={{32,24},{24,16},{16,8},{8,0},{33,25},{25,17},{17,9},{9,1},{34,26},... | collective-permute-start | bytes 196616 | tf_op jit(solution)/shard_map/ppermute | solution.py:200
  355.1 95.9 %collective-permute-start.94 = (bf16[64,512]{1,0:T(8,128)(2,1)S(1)}, bf16[64,512]{1,0:T(8,128)(2,1)S(1)}, u32[]{:S(2)}, u32[]{:S(2)}) collective-permute-start(bf16[64,512]{1,0:T(8,128)(2,1)S(1)} %bwd.94), channel_id=1, source_target_pairs={{32,24},{24,16},{16,8},{8,0},{33,25},{25,17},{17,9},{9,1},{34,26},... | collective-permute-start | bytes 196616 | tf_op jit(solution)/shard_map/ppermute | solution.py:200
  449.1 6.6 %collective-permute-start.127 = (bf16[64,512]{1,0:T(8,128)(2,1)S(1)}, bf16[64,512]{1,0:T(8,128)(2,1)S(1)}, u32[]{:S(2)}, u32[]{:S(2)}) collective-permute-start(bf16[64,512]{1,0:T(8,128)(2,1)S(1)} %bwd.127), channel_id=1, source_target_pairs={{32,24},{24,16},{16,8},{8,0},{33,25},{25,17},{17,9},{9,1},{34,26},... | collective-permute-start | bytes 196616 | tf_op jit(solution)/shard_map/ppermute | solution.py:200
  452.6 6.6 %collective-permute-start.95 = (bf16[64,512]{1,0:T(8,128)(2,1)S(1)}, bf16[64,512]{1,0:T(8,128)(2,1)S(1)}, u32[]{:S(2)}, u32[]{:S(2)}) collective-permute-start(bf16[64,512]{1,0:T(8,128)(2,1)S(1)} %bwd.95), channel_id=1, source_target_pairs={{32,24},{24,16},{16,8},{8,0},{33,25},{25,17},{17,9},{9,1},{34,26},... | collective-permute-start | bytes 196616 | tf_op jit(solution)/shard_map/ppermute | solution.py:200
  (133 other events, 487.3 us)
Sparse Core Ops, SparseCore 0:
  195.9 98.5 all-gather.2
  460.3 88.7 all-gather.4

commit v4 on v2

--- a/solution.py
+++ b/solution.py
@@ -202,6 +202,7 @@
     sig = sigmoid(pre)
     hidden = (pre * sig).astype(jnp.bfloat16)
     slope = sig + pre * sig * (1.0 - sig)
+    hidden, slope = lax.optimization_barrier((hidden, slope))
     through = jnp.einsum("rd,fd->rf", all_grads, out_part, preferred_element_type=jnp.float32)
     grad_pre = (through * slope).astype(jnp.bfloat16)
     share_in = jnp.einsum("rd,rf->df", all_acts, grad_pre, preferred_element_type=jnp.float32)

time: 576 us -> 575 us (level)
  transfers between devices with their start and end apart: 70 -> 70, of which waited for: 9 -> 9; matrix products, arithmetic and copies ran while one was open for 1% -> 2% of each run, Pallas kernels for 10% -> 10%
where the time goes in v4:
time: 575 us; the launch traced here: 565 us
  waiting for transfers between devices  334 us (58%)
  Pallas kernels  117 us (20%)
  starting transfers between devices  62.5 us (11%)
  matrix products  17.4 us (3%)
  between operations  17 us (3%)
  local copies, waits for them, and re-layouts  15.2 us (3%)
    ppermute x34, waiting for transfers between devices, per_device(): grad = lax.ppermute(out, 'section', pairs)  250 us
    all_gather x1, waiting for transfers between devices, per_device(): lax.all_gather(grads.reshape(micro * rows, width), 'dp', tiled=True)  78.1 us
    pallas_call x35, Pallas kernels, per_device(): out = forward(act, weight_in, weight_out)  57.4 us
    pallas_call x34, Pallas kernels, per_device(): out = backward(tick)(sec_arr, grad, slopes, *turned)  54.2 us
    ppermute x34, starting transfers between devices, per_device(): act = lax.ppermute(out, 'section', pairs)  36.2 us
    ppermute x34, starting transfers between devices, per_device(): grad = lax.ppermute(out, 'section', pairs)  26.2 us
    unnamed x120, local copies, waits for them, and re-layouts  15.2 us
  transfers between devices with their start and end apart: 70, of which 9 were waited for; matrix products, arithmetic and copies ran while one was open for 2% of the time, Pallas kernels for 10%

profile of v4, /device:TPU:1, one launch (start us, length us, event | category | flops | bytes accessed | tf_op | source)
XLA Modules:
  0.0 565.1 jit_solution(5151608998991564749)
XLA Ops:
  8.2 2.2 copy-done
  10.4 2.2 copy-done.2
  14.2 4.4 collective-permute-start
  21.6 3.7 collective-permute-start.1
  28.2 3.7 collective-permute-start.2
  34.9 3.7 collective-permute-start.3
  42.6 1.8 copy-done.1
  66.1 1.6 fwd.48
  70.8 1.6 fwd.50
  75.5 1.6 fwd.52
  80.4 1.6 fwd.54
  85.1 1.6 fwd.56
  89.7 1.6 fwd.58
  104.0 1.6 fwd.64
  115.9 2.3 slope.1.slope_ref
  123.4 2.2 copy-done.5
  202.2 234.6 %collective-permute-done.64.grad_ref = bf16[64,512]{1,0:T(8,128)(2,1)S(1)} collective-permute-done((bf16[64,512]{1,0:T(8,128)(2,1)S(1)}, bf16[64,512]{1,0:T(8,128)(2,1)S(1)}, u32[]{:S(2)}, u32[]{:S(2)}) %collective-permute-start.64) | collective-permute-done | bytes 65568 | tf_op jit(solution)/shard_map/ppermute | solution.py:187
  439.9 5.6 collective-permute-done.65.grad_ref
  448.4 5.8 %collective-permute-done.66.grad_ref = bf16[64,512]{1,0:T(8,128)(2,1)S(1)} collective-permute-done((bf16[64,512]{1,0:T(8,128)(2,1)S(1)}, bf16[64,512]{1,0:T(8,128)(2,1)S(1)}, u32[]{:S(2)}, u32[]{:S(2)}) %collective-permute-start.66) | collective-permute-done | bytes 65568 | tf_op jit(solution)/shard_map/ppermute | solution.py:187
  457.1 4.3 collective-permute-done.67
  462.3 6.5 %multiply_add_fusion = (f32[2048,512]{1,0:T(8,128)}, bf16[2048,512]{1,0:T(8,128)(2,1)}) fusion(bf16[2048,512]{1,0:T(8,128)(2,1)} %all-gather.3.cloned.1.call-done, bf16[1,512,4096]{2,1,0:T(8,128)(2,1)} %param.6, u32[]{:T(128)S(6)} %convert_element_type.29), kind=kOutput, calls=%fused_computation.1 | convolution fusion | flops 1082130432 | bytes 8912900 | tf_op jit(solution)/shard_map/dot_general | solution.py:201
  468.8 78.1 %all-gather.5.cloned.1.call-done = bf16[2048,512]{1,0:T(8,128)(2,1)} async-done(((bf16[256,512]{1,0:T(8,128)(2,1)}), bf16[2048,512]{1,0:T(8,128)(2,1)}) %all-gather.5.cloned.1.call-update) | async-done | bytes 2097168 | tf_op jit(solution)/shard_map/all_gather | solution.py:200
  546.9 4.5 convolution_bitcast_fusion
  551.4 6.4 %convolution_bitcast_fusion.1 = f32[1,512,512]{2,1,0:T(8,128)} fusion(bf16[2048,512]{1,0:T(8,128)(2,1)S(1)} %copy-done.26, f32[2048,512]{1,0:T(8,128)} %get-tuple-element.50, bf16[2048,512]{1,0:T(8,128)(2,1)} %all-gather.5.cloned.1.call-done, bf16[1,4096,512]{2,1,0:T(8,128)(2,1)} %param.7, u32[]{:T(128)S(6)} %convert_element_type.29), kind=kOutput, calls=%fused_computation.6 | convolution fusion | flops 2149580800 | bytes 9961476 | tf_op jit(solution)/shard_map/rd,rf->df/dot_general | solution.py:208
  (332 shorter events, 164.8 us)
Async XLA Ops:
  7.2 455.1 %all-gather.3.cloned.1.call-start = ((), (), s32[]{:S(2)}) async-start(), calls=%async_computation | async-start | bytes 2359296 | tf_op jit(solution)/shard_map/all_gather | solution.py:199
  14.2 5.7 %collective-permute-start = (bf16[64,512]{1,0:T(8,128)(2,1)S(1)}, bf16[64,512]{1,0:T(8,128)(2,1)S(1)}, u32[]{:S(2)}, u32[]{:S(2)}) collective-permute-start(bf16[64,512]{1,0:T(8,128)(2,1)S(1)} %fwd.35), channel_id=1, source_target_pairs={{0,8},{8,16},{1,9},{9,17},{2,10},{10,18},{3,11},{11,19},{4,12},{12... | collective-permute-start | bytes 196616 | tf_op jit(solution)/shard_map/ppermute | solution.py:159
  21.6 5.0 collective-permute-start.1
  28.2 5.0 collective-permute-start.2
  34.9 5.0 collective-permute-start.3
  41.6 1.1 collective-permute-start.4
  46.1 1.0 collective-permute-start.5
  48.8 1.0 collective-permute-start.6
  51.5 1.1 collective-permute-start.7
  54.2 1.5 collective-permute-start.8
  57.4 1.0 collective-permute-start.9
  60.0 1.0 collective-permute-start.10
  62.7 1.0 collective-permute-start.11
  77.1 0.9 collective-permute-start.17
  100.8 0.9 collective-permute-start.27
  121.8 0.7 collective-permute-start.34
  122.5 424.5 %all-gather.5.cloned.1.call-start = ((), (), s32[]{:S(2)}) async-start(), calls=%async_computation.1 | async-start | bytes 2359296 | tf_op jit(solution)/shard_map/all_gather | solution.py:200
  133.3 1.1 collective-permute-start.35
  156.8 0.9 collective-permute-start.45
  179.9 0.9 collective-permute-start.55
  200.8 235.9 %collective-permute-start.64 = (bf16[64,512]{1,0:T(8,128)(2,1)S(1)}, bf16[64,512]{1,0:T(8,128)(2,1)S(1)}, u32[]{:S(2)}, u32[]{:S(2)}) collective-permute-start(bf16[64,512]{1,0:T(8,128)(2,1)S(1)} %bwd.64), channel_id=1, source_target_pairs={{32,24},{24,16},{16,8},{8,0},{33,25},{25,17},{17,9},{9,1},{34,26},... | collective-permute-start | bytes 196616 | tf_op jit(solution)/shard_map/ppermute | solution.py:187
  438.4 7.1 %collective-permute-start.65 = (bf16[64,512]{1,0:T(8,128)(2,1)S(1)}, bf16[64,512]{1,0:T(8,128)(2,1)S(1)}, u32[]{:S(2)}, u32[]{:S(2)}) collective-permute-start(bf16[64,512]{1,0:T(8,128)(2,1)S(1)} %bwd.65), channel_id=1, source_target_pairs={{32,24},{24,16},{16,8},{8,0},{33,25},{25,17},{17,9},{9,1},{34,26},... | collective-permute-start | bytes 196616 | tf_op jit(solution)/shard_map/ppermute | solution.py:187
  447.1 7.1 %collective-permute-start.66 = (bf16[64,512]{1,0:T(8,128)(2,1)S(1)}, bf16[64,512]{1,0:T(8,128)(2,1)S(1)}, u32[]{:S(2)}, u32[]{:S(2)}) collective-permute-start(bf16[64,512]{1,0:T(8,128)(2,1)S(1)} %bwd.66), channel_id=1, source_target_pairs={{16,8},{8,0},{17,9},{9,1},{18,10},{10,2},{19,11},{11,3},{20,12},{1... | collective-permute-start | bytes 196616 | tf_op jit(solution)/shard_map/ppermute | solution.py:187
  455.8 5.6 collective-permute-start.67
  (73 other events, 500.1 us)
Sparse Core Ops, SparseCore 0:
  122.6 175.2 all-gather.2
  462.4 84.4 all-gather.4
